TPU v7x, 256 devices: a whole 4x4x8 slice. The times are simulated.
256 devices in a mesh: row: 32 (over x, y, core), col: 8 (over z).
Axes of the slice: x: 4, y: 4, z: 8, core: 2. Of those that a mesh axis runs over, the one named last changes fastest.
Arguments:
- activations: float32 [32768, 8192], P('row', 'col'), may hold values from -120 to 120
- plan: int32 [2, 32], replicated, may hold values from 0 to 31, as said below
Outputs:
- rotated: float32 [32768, 8192], P('row', 'col')
Inputs may be any that keep to these rules, and one draw needn't show every extreme that they name: `plan`: row r gives, for every slot, which block of layout 0 stands there in round r; row 0 is the identity and each row is a permutation. Going from one round to the next, all blocks but the one in a fixed slot move one place along the circle of slots formed by the leads in rising order followed by the mates in falling order (the fixed slot is skipped), all in the same sense, so each index of col sends at most one block to each neighbouring index and none farther.
All inputs are finite; a program needn't handle non-finite values.
Results may differ from a plain program's by a relative error of at most 0.0003.
Values sent between devices are 32-bit elements; how exact they have to be, the bound alone decides.
A program may use at most 128 MiB of HBM per device.

v0:
```python
import jax
import jax.numpy as jnp
from jax import lax
from jax.sharding import PartitionSpec as P

BLK = 256
ROUNDS = 2


highest = lax.Precision.HIGHEST
epsilon = 1e-06


def shifted(value, axis, by):
    size = lax.axis_size(axis)
    pairs = [(i, i + by) for i in range(size) if 0 <= i + by < size]
    return lax.ppermute(value, axis, pairs)


def inverse_spd(matrix):
    factor = jnp.linalg.cholesky(matrix)
    unit_batch = jnp.broadcast_to(jnp.eye(matrix.shape[-1], dtype=matrix.dtype), matrix.shape)
    inverse_factor = jax.scipy.linalg.solve_triangular(factor, unit_batch, lower=True)
    return jnp.einsum("pba,pbc->pac", inverse_factor, inverse_factor, precision=highest)


def cayley_update(lead_block, mate_block, cross_gram, lead_sq, mate_sq):
    coupling = cross_gram / (lead_sq[:, :, None] + mate_sq[:, None, :] + epsilon)
    identity = jnp.eye(coupling.shape[-1], dtype=jnp.float32)[None, :, :]
    left_gram = identity + 0.25 * jnp.einsum("pab,pcb->pac", coupling, coupling, precision=highest)
    right_gram = identity + 0.25 * jnp.einsum("pba,pbc->pac", coupling, coupling, precision=highest)
    left_inv = inverse_spd(left_gram)
    right_inv = inverse_spd(right_gram)
    mixed_lead = 2.0 * lead_block - jnp.einsum(
        "rpb,pab->rpa", mate_block, coupling, precision=highest
    )
    mixed_mate = (
        jnp.einsum("rpa,pab->rpb", lead_block, coupling, precision=highest) + 2.0 * mate_block
    )
    new_lead = jnp.einsum("rpa,pab->rpb", mixed_lead, left_inv, precision=highest) - lead_block
    new_mate = jnp.einsum("rpa,pab->rpb", mixed_mate, right_inv, precision=highest) - mate_block
    return (new_lead, new_mate)


def local_sums(lead_block, mate_block):
    cross_gram = jnp.einsum("rpa,rpb->pab", lead_block, mate_block, precision=highest)
    lead_sq = jnp.sum(lead_block * lead_block, axis=0)
    mate_sq = jnp.sum(mate_block * mate_block, axis=0)
    return (cross_gram, lead_sq, mate_sq)


def source_slots(earlier_layout, later_layout):
    slot_total = earlier_layout.shape[0]
    matches = later_layout[:, None] == earlier_layout[None, :]
    positions = jnp.arange(slot_total, dtype=jnp.int32)
    return jnp.sum(jnp.where(matches, positions[None, :], 0), axis=1)


def relocate(current, earlier_layout, later_layout):
    row_count = current.shape[0]
    local_slots = current.shape[1] // BLK
    device = lax.axis_index("col")
    base = device * local_slots
    source = source_slots(earlier_layout, later_layout)
    target = source_slots(later_layout, earlier_layout)
    incoming = lax.dynamic_slice_in_dim(source, base, local_slots)
    outgoing = lax.dynamic_slice_in_dim(target, base, local_slots)
    source_device = incoming // local_slots
    target_device = outgoing // local_slots
    local_blocks = current.reshape(row_count, local_slots, BLK)
    to_lower = target_device == device - 1
    to_upper = target_device == device + 1
    send_lower = jnp.sum(jnp.where(to_lower[None, :, None], local_blocks, 0.0), axis=1)
    send_upper = jnp.sum(jnp.where(to_upper[None, :, None], local_blocks, 0.0), axis=1)
    from_upper = shifted(send_lower, "col", -1)
    from_lower = shifted(send_upper, "col", 1)
    candidates = jnp.concatenate(
        [local_blocks, from_upper[:, None, :], from_lower[:, None, :]], axis=1
    )
    chosen = jnp.where(
        source_device == device,
        incoming - base,
        jnp.where(source_device == device + 1, local_slots, local_slots + 1),
    )
    moved = jnp.take(candidates, chosen, axis=1)
    return moved.reshape(row_count, local_slots * BLK)


def shards(activations, plan):
    row_count = activations.shape[0]
    local_slots = activations.shape[1] // BLK
    pair_count = local_slots // 2
    current = activations
    for round_index in range(ROUNDS):
        blocks = current.reshape(row_count, pair_count, 2, BLK)
        lead_block = blocks[:, :, 0, :]
        mate_block = blocks[:, :, 1, :]
        cross_gram, lead_sq, mate_sq = local_sums(lead_block, mate_block)
        cross_gram, lead_sq, mate_sq = lax.psum((cross_gram, lead_sq, mate_sq), "row")
        new_lead, new_mate = cayley_update(lead_block, mate_block, cross_gram, lead_sq, mate_sq)
        current = jnp.stack([new_lead, new_mate], axis=2).reshape(row_count, local_slots * BLK)
        if round_index + 1 < ROUNDS:
            current = relocate(current, plan[round_index], plan[round_index + 1])
    return current


def solution(mesh):
    placed = (P("row", "col"), P())
    return jax.shard_map(
        shards, mesh=mesh, in_specs=placed, out_specs=P("row", "col"), check_vma=False
    )
```

profile of v0, /device:TPU:1, one launch (start us, length us, event | category | flops | bytes accessed | tf_op | source)
XLA Modules:
  0.0 832.6 jit_solution(7184385660625403359)
XLA Ops:
  6.5 5.3 copy.89
  11.9 5.1 fusion.2
  17.1 4.0 fusion.95
  31.0 65.4 %all-reduce.2 = (f32[2,256]{1,0:T(2,128)S(1)}, f32[2,256]{1,0:T(2,128)S(1)}) all-reduce(f32[2,256]{1,0:T(2,128)S(1)} %get-tuple-element.128, f32[2,256]{1,0:T(2,128)S(1)} %get-tuple-element.129), channel_id=1, replica_groups=mesh['row'=32,'col'=8] {'row'}, use_global_device_ids=true, to_apply=%region_5.6 | all-reduce | flops 1024 | bytes 8192 | tf_op jit(solution)/shard_map/psum | solution.py:99
  96.5 38.1 %all-reduce.6.cloned.1.call-done = f32[2,256,256]{2,1,0:T(8,128)} async-done(((f32[2,256,256]{2,1,0:T(8,128)}), f32[2,256,256]{2,1,0:T(8,128)}) %all-reduce.6.cloned.1.call-update) | async-done | bytes 524304 | tf_op jit(solution)/shard_map/psum | solution.py:99
  134.6 2.4 fusion.24
  138.2 23.5 %custom-call.29 = f32[2,128,128]{2,1,0:T(8,128)S(1)} custom-call(f32[2,128,128]{2,1,0:T(8,128)S(1)} %cholesky.353), custom_call_target="Cholesky" | custom-call | tf_op jit(solution)/shard_map/jit(cholesky)/cholesky | solution.py:21
  161.6 2.1 fusion.25
  164.8 23.5 %custom-call.25 = f32[2,128,128]{2,1,0:T(8,128)S(1)} custom-call(f32[2,128,128]{2,1,0:T(8,128)S(1)} %cholesky.350), custom_call_target="Cholesky" | custom-call | tf_op jit(solution)/shard_map/jit(cholesky)/cholesky | solution.py:21
  189.1 19.9 %custom-call.30 = f32[2,1,128,128]{2,3,1,0:T(8,128)S(1)} custom-call(f32[2,1,128,128]{3,2,1,0:T(8,128)S(1)} %get-tuple-element.115), custom_call_target="InvertDiagBlocksLowerTriangular" | custom-call | tf_op jit(solution)/shard_map/jit(cholesky)/cholesky | solution.py:21
  211.5 24.1 %custom-call.31 = f32[2,128,128]{2,1,0:T(8,128)} custom-call(f32[2,128,128]{2,1,0:T(8,128)S(1)} %convolution_subtract_fusion.6), custom_call_target="Cholesky" | custom-call | tf_op jit(solution)/shard_map/jit(cholesky)/cholesky | solution.py:21
  235.6 20.3 %custom-call.26 = f32[2,1,128,128]{2,3,1,0:T(8,128)} custom-call(f32[2,1,128,128]{3,2,1,0:T(8,128)S(1)} %get-tuple-element.114), custom_call_target="InvertDiagBlocksLowerTriangular" | custom-call | tf_op jit(solution)/shard_map/jit(cholesky)/cholesky | solution.py:21
  260.0 25.3 %custom-call.27 = f32[2,128,128]{2,1,0:T(8,128)} custom-call(f32[2,128,128]{2,1,0:T(8,128)} %convolution_subtract_fusion.7), custom_call_target="Cholesky" | custom-call | tf_op jit(solution)/shard_map/jit(cholesky)/cholesky | solution.py:21
  289.6 5.2 while.8
  294.8 40.7 %custom-call.28 = f32[2,2,128,128]{2,3,1,0:T(8,128)} custom-call(f32[2,2,128,128]{3,2,1,0:T(8,128)} %bitcast.272), custom_call_target="InvertDiagBlocksLowerTriangular" | custom-call | tf_op jit(solution)/shard_map/jit(_solve_triangular)/vmap()/triangular_solve | solution.py:23
  340.7 4.0 while.9
  344.7 39.5 %custom-call.32 = f32[2,2,128,128]{2,3,1,0:T(8,128)S(1)} custom-call(f32[2,2,128,128]{3,2,1,0:T(8,128)S(1)} %bitcast.273), custom_call_target="InvertDiagBlocksLowerTriangular" | custom-call | tf_op jit(solution)/shard_map/jit(_solve_triangular)/vmap()/triangular_solve | solution.py:23
  388.3 5.4 fusion
  393.8 2.0 fusion.13
  396.1 3.7 fusion.4
  399.8 2.3 fusion.11
  402.2 3.8 select_reduce_fusion.1
  407.2 4.1 collective-permute-start.1
  411.5 2.5 copy.123
  414.0 17.9 %collective-permute-done = f32[1024,256]{1,0:T(8,128)S(1)} collective-permute-done((f32[1024,256]{1,0:T(8,128)}, f32[1024,256]{1,0:T(8,128)S(1)}, u32[]{:S(2)}, u32[]{:S(2)}) %collective-permute-start) | collective-permute-done | bytes 1048608 | tf_op jit(solution)/shard_map/ppermute | solution.py:17
  432.6 3.2 pad_maximum_fusion
  435.8 5.6 gather_fusion
  441.4 2.7 copy_select_fusion
  446.1 4.3 fusion.20
  450.5 2.6 multiply_reduce_fusion.1
  453.0 64.4 %all-reduce.1 = (f32[2,256]{1,0:T(2,128)S(1)}, f32[2,256]{1,0:T(2,128)S(1)}) all-reduce(f32[2,256]{1,0:T(2,128)S(1)} %get-tuple-element.38, f32[2,256]{1,0:T(2,128)S(1)} %get-tuple-element.37), channel_id=1, replica_groups=mesh['row'=32,'col'=8] {'row'}, use_global_device_ids=true, to_apply=%region_17.20 | all-reduce | flops 1024 | bytes 8192 | tf_op jit(solution)/shard_map/psum | solution.py:99
  517.4 50.1 %all-reduce.8.cloned.1.call-done = f32[2,256,256]{2,1,0:T(8,128)} async-done(((f32[2,256,256]{2,1,0:T(8,128)}), f32[2,256,256]{2,1,0:T(8,128)}) %all-reduce.8.cloned.1.call-update) | async-done | bytes 524304 | tf_op jit(solution)/shard_map/psum | solution.py:99
  567.5 2.5 fusion.22
  570.3 23.5 %custom-call.37 = f32[2,128,128]{2,1,0:T(8,128)S(1)} custom-call(f32[2,128,128]{2,1,0:T(8,128)S(1)} %cholesky.359), custom_call_target="Cholesky" | custom-call | tf_op jit(solution)/shard_map/jit(cholesky)/cholesky | solution.py:21
  595.0 23.5 %custom-call.33 = f32[2,128,128]{2,1,0:T(8,128)S(1)} custom-call(f32[2,128,128]{2,1,0:T(8,128)S(1)} %cholesky.356), custom_call_target="Cholesky" | custom-call | tf_op jit(solution)/shard_map/jit(cholesky)/cholesky | solution.py:21
  619.2 19.8 %custom-call.38 = f32[2,1,128,128]{2,3,1,0:T(8,128)S(1)} custom-call(f32[2,1,128,128]{3,2,1,0:T(8,128)S(1)} %get-tuple-element.113), custom_call_target="InvertDiagBlocksLowerTriangular" | custom-call | tf_op jit(solution)/shard_map/jit(cholesky)/cholesky | solution.py:21
  639.7 23.5 %custom-call.39 = f32[2,128,128]{2,1,0:T(8,128)S(1)} custom-call(f32[2,128,128]{2,1,0:T(8,128)S(1)} %convolution_subtract_fusion.4), custom_call_target="Cholesky" | custom-call | tf_op jit(solution)/shard_map/jit(cholesky)/cholesky | solution.py:21
  663.2 19.7 %custom-call.34 = f32[2,1,128,128]{2,3,1,0:T(8,128)S(1)} custom-call(f32[2,1,128,128]{3,2,1,0:T(8,128)S(1)} %get-tuple-element.112), custom_call_target="InvertDiagBlocksLowerTriangular" | custom-call | tf_op jit(solution)/shard_map/jit(cholesky)/cholesky | solution.py:21
  683.6 23.7 %custom-call.35 = f32[2,128,128]{2,1,0:T(8,128)S(1)} custom-call(f32[2,128,128]{2,1,0:T(8,128)S(1)} %convolution_subtract_fusion.5), custom_call_target="Cholesky" | custom-call | tf_op jit(solution)/shard_map/jit(cholesky)/cholesky | solution.py:21
  708.9 5.4 while.10
  714.3 39.3 %custom-call.36 = f32[2,2,128,128]{2,3,1,0:T(8,128)S(1)} custom-call(f32[2,2,128,128]{3,2,1,0:T(8,128)S(1)} %bitcast.274), custom_call_target="InvertDiagBlocksLowerTriangular" | custom-call | tf_op jit(solution)/shard_map/jit(_solve_triangular)/vmap()/triangular_solve | solution.py:23
  756.2 4.1 while.11
  760.3 39.6 %custom-call.40 = f32[2,2,128,128]{2,3,1,0:T(8,128)S(1)} custom-call(f32[2,2,128,128]{3,2,1,0:T(8,128)S(1)} %bitcast.271), custom_call_target="InvertDiagBlocksLowerTriangular" | custom-call | tf_op jit(solution)/shard_map/jit(_solve_triangular)/vmap()/triangular_solve | solution.py:23
  802.4 3.8 fusion.21
  808.2 2.2 fusion.19
  812.4 2.3 pad_maximum_fusion.2
  814.7 5.4 copy.158
  820.1 5.3 copy.159
  (178 shorter events, 70.0 us)
Async XLA Ops:
  6.5 128.1 %all-reduce.6.cloned.1.call-start = ((), (), s32[]{:S(2)}) async-start(), calls=%async_computation | async-start | bytes 1048576 | tf_op jit(solution)/shard_map/psum | solution.py:99
  17.0 550.5 %all-reduce.8.cloned.1.call-start = ((), (), s32[]{:S(2)}) async-start(), calls=%async_computation.1 | async-start | bytes 1048576 | tf_op jit(solution)/shard_map/psum | solution.py:99
  21.1 113.5 %copy-start.12 = (f32[256,256]{0,1:T(8,128)}, f32[256,256]{0,1:T(8,128)S(1)}, u32[]{:S(2)}) copy-start(f32[256,256]{0,1:T(8,128)S(1)} %fusion.50) | copy-start | bytes 786436
  24.3 1.9 copy-start.24
  96.5 40.9 %copy-start.19 = (f32[2,256]{1,0:T(2,128)}, f32[2,256]{1,0:T(2,128)S(1)}, u32[]{:S(2)}) copy-start(f32[2,256]{1,0:T(2,128)S(1)} %get-tuple-element.85) | copy-start | bytes 6148
  96.5 40.9 %copy-start.21 = (f32[2,256]{1,0:T(2,128)}, f32[2,256]{1,0:T(2,128)S(1)}, u32[]{:S(2)}) copy-start(f32[2,256]{1,0:T(2,128)S(1)} %get-tuple-element.86) | copy-start | bytes 6148
  137.3 0.8 copy-start.10
  164.0 0.8 copy-start.9
  188.3 0.8 copy-start.11
  285.3 3.5 copy-start.30
  286.4 0.8 copy-start.4
  286.4 1.0 copy-start.5
  340.7 47.6 %copy-start.20 = (f32[2,256]{1,0:T(2,128)S(1)}, f32[2,256]{1,0:T(2,128)}, u32[]{:S(2)}) copy-start(f32[2,256]{1,0:T(2,128)} %copy-done.19) | copy-start | bytes 6148
  340.7 47.6 %copy-start.22 = (f32[2,256]{1,0:T(2,128)S(1)}, f32[2,256]{1,0:T(2,128)}, u32[]{:S(2)}) copy-start(f32[2,256]{1,0:T(2,128)} %copy-done.21) | copy-start | bytes 6148
  344.7 49.1 %copy-start.28 = (s32[2,2]{1,0:T(2,128)}, s32[2,2]{1,0:T(2,128)S(1)}, u32[]{:S(2)}) copy-start(s32[2,2]{1,0:T(2,128)S(1)} %get-tuple-element.322) | copy-start | bytes 52
  384.2 0.7 copy-start.14
  388.3 5.5 copy-start.3
  388.3 5.5 copy-start.6
  393.8 2.2 copy-start.2
  393.8 2.3 copy-start.7
  399.8 2.4 copy-start.25
  399.8 2.4 copy-start.26
  402.1 9.1 %copy-start.27 = (pred[4]{0:T(512)(128)(4,1)S(1)}, pred[4]{0:T(512)(128)(4,1)}, u32[]{:S(2)}) copy-start(pred[4]{0:T(512)(128)(4,1)} %get-tuple-element.87) | copy-start | bytes 16
  402.2 9.3 %copy-start.23 = (s32[4]{0:T(128)S(1)}, s32[4]{0:T(128)}, u32[]{:S(2)}) copy-start(s32[4]{0:T(128)} %get-tuple-element.88) | copy-start | bytes 52
  405.9 26.0 %collective-permute-start = (f32[1024,256]{1,0:T(8,128)}, f32[1024,256]{1,0:T(8,128)S(1)}, u32[]{:S(2)}, u32[]{:S(2)}) collective-permute-start(f32[1024,256]{1,0:T(8,128)} %get-tuple-element.39), channel_id=1, source_target_pairs={{1,0},{2,1},{3,2},{4,3},{5,4},{6,5},{7,6},{9,8},{10,9},{11,10},{12... | collective-permute-start | bytes 3145736 | tf_op jit(solution)/shard_map/ppermute | solution.py:17
  407.2 25.4 %collective-permute-start.1 = (f32[1024,256]{1,0:T(8,128)S(1)}, f32[1024,256]{1,0:T(8,128)S(1)}, u32[]{:S(2)}, u32[]{:S(2)}) collective-permute-start(f32[1024,256]{1,0:T(8,128)S(1)} %get-tuple-element.40), channel_id=1, source_target_pairs={{0,1},{1,2},{2,3},{3,4},{4,5},{5,6},{6,7},{8,9},{9,10},{10,11},{11... | collective-permute-start | bytes 3145736 | tf_op jit(solution)/shard_map/ppermute | solution.py:17
  444.1 2.0 copy-start
  450.5 117.1 %copy-start.13 = (f32[256,256]{0,1:T(8,128)S(1)}, f32[256,256]{0,1:T(8,128)}, u32[]{:S(2)}) copy-start(f32[256,256]{0,1:T(8,128)} %copy-done.12) | copy-start | bytes 786436
  517.4 76.4 %copy-start.15 = (f32[2,256]{1,0:T(2,128)}, f32[2,256]{1,0:T(2,128)S(1)}, u32[]{:S(2)}) copy-start(f32[2,256]{1,0:T(2,128)S(1)} %get-tuple-element.83) | copy-start | bytes 6148
  517.4 76.4 %copy-start.17 = (f32[2,256]{1,0:T(2,128)}, f32[2,256]{1,0:T(2,128)S(1)}, u32[]{:S(2)}) copy-start(f32[2,256]{1,0:T(2,128)S(1)} %get-tuple-element.84) | copy-start | bytes 6148
  567.5 26.3 %copy-start.8 = (f32[2,256,256]{2,1,0:T(8,128)S(1)}, f32[2,256,256]{2,1,0:T(8,128)}, u32[]{:S(2)}) copy-start(f32[2,256,256]{2,1,0:T(8,128)} %all-reduce.8.cloned.1.call-done) | copy-start | bytes 1572868
  714.3 41.9 %copy-start.29 = (s32[2,2]{1,0:T(2,128)S(1)}, s32[2,2]{1,0:T(2,128)}, u32[]{:S(2)}) copy-start(s32[2,2]{1,0:T(2,128)} %get-tuple-element.323) | copy-start | bytes 52
  756.2 46.2 %copy-start.16 = (f32[2,256]{1,0:T(2,128)S(1)}, f32[2,256]{1,0:T(2,128)}, u32[]{:S(2)}) copy-start(f32[2,256]{1,0:T(2,128)} %copy-done.15) | copy-start | bytes 6148
  756.2 46.2 %copy-start.18 = (f32[2,256]{1,0:T(2,128)S(1)}, f32[2,256]{1,0:T(2,128)}, u32[]{:S(2)}) copy-start(f32[2,256]{1,0:T(2,128)} %copy-done.17) | copy-start | bytes 6148
  802.4 3.8 copy-start.1
Sparse Core Ops, SparseCore 0:
  17.1 117.4 all-reduce.5
  450.6 116.8 all-reduce.7
where the time goes:
time: 837 us; the launch traced here: 833 us
  other arithmetic  455 us (54%)
  blocking collectives  130 us (16%)
  waiting for transfers between devices  107 us (13%)
  matrix products  61.1 us (7%)
  local copies, waits for them, and re-layouts  60 us (7%)
  between operations  14.6 us (2%)
    another operation x30, other arithmetic, inverse_spd(): factor = jnp.linalg.cholesky(matrix)  274 us
    another operation x8, other arithmetic, inverse_spd(): jax.scipy.linalg.solve_triangular(factor, unit_batch, lower=True)  163 us
    psum x2, blocking collectives, shards(): lax.psum((cross_gram, lead_sq, mate_sq), 'row')  130 us
    psum x2, waiting for transfers between devices, shards(): lax.psum((cross_gram, lead_sq, mate_sq), 'row')  88.2 us
    another operation x30, local copies, waits for them, and re-layouts, inverse_spd(): jax.scipy.linalg.solve_triangular(factor, unit_batch, lower=True)  19.3 us
    ppermute x2, waiting for transfers between devices, shifted(): return lax.ppermute(value, axis, pairs)  18.6 us
  transfers between devices with their start and end apart: 4, of which 4 were waited for; matrix products, arithmetic and copies ran while one was open for 2% of the time, Pallas kernels for 0%

commit v1 on v0

v1 whole, which is shorter than its diff:
```python
import functools

import jax
import jax.numpy as jnp
from jax import lax
from jax.experimental import pallas as pl
from jax.experimental.pallas import tpu as pltpu
from jax.sharding import PartitionSpec as P

BLK = 256
HALF = 128
EPS = 1e-6
STEPS = 9
BOUND = 1.02 * (1.0 + (BLK / 2) ** 2 / 4)
MESH = pl.DeviceIdType.MESH
HIGHEST = lax.Precision.HIGHEST
f32, bf16 = jnp.float32, jnp.bfloat16


def split(value):
    hi = value.astype(bf16)
    return hi, (value - hi.astype(f32)).astype(bf16)


def mm(a, b):
    return lax.dot_general(a, b, (((1,), (0,)), ((), ())), preferred_element_type=f32)


def mm_t(a, b):
    return lax.dot_general(a, b, (((0,), (0,)), ((), ())), preferred_element_type=f32)


def mm3(a, b):
    return mm(a[0], b[0]) + (mm(a[0], b[1]) + mm(a[1], b[0]))


def full(a, b, dims):
    return lax.dot_general(a, b, (dims, ((), ())), precision=HIGHEST, preferred_element_type=f32)


def eye():
    rows = lax.broadcasted_iota(jnp.int32, (BLK, BLK), 0)
    cols = lax.broadcasted_iota(jnp.int32, (BLK, BLK), 1)
    return jnp.where(rows == cols, 1.0, 0.0).astype(f32)


def put_rotation(q, hi_ref, lo_ref, pair):
    q11, w, q22 = q
    for value, r, c in ((q11, 0, 0), (w, 0, 1), (-w.T, 1, 0), (q22, 1, 1)):
        hi, lo = split(value)
        hi_ref[pair, r * BLK : (r + 1) * BLK, c * BLK : (c + 1) * BLK] = hi
        lo_ref[pair, r * BLK : (r + 1) * BLK, c * BLK : (c + 1) * BLK] = lo


def rounds_kernel(
    n_row, n_col, rows, step_rows,
    plan_ref, x_ref, x2_ref, q_ref,
    xv, nv, zsend, zrecv, gram, sq, part_send, part_recv, rs_src, rs_recv, ag, rx, gmat, cmat, qv, qhi, qlo,
    load_sem, part_s, part_r, rs_s, rs_r, ag_s, ag_r, q_s, q_r, z_s, z_r, out_sem,
):
    chips = n_row // 2
    crow = BLK // chips
    row, z = lax.axis_index("row"), lax.axis_index("col")
    core, chip = lax.rem(row, 2), row // 2
    other = 1 - core
    partner = (chip * 2 + other, z)
    z_up, z_down = lax.rem(z + 1, n_col), lax.rem(z + n_col - 1, n_col)
    n_steps = rows // step_rows

    def peer(k):
        t = lax.rem(chip + k, chips)
        return t, (t * 2 + core, z)

    loads = []
    for i, p in enumerate((other, core)):
        for h in range(2):
            cols = pl.ds(pl.multiple_of((2 * p + h) * BLK, BLK), BLK)
            loads.append(pltpu.make_async_copy(x_ref.at[:, cols], xv.at[2 * p + h], load_sem.at[2 * i + h]))
            loads[-1].start()

    barrier = pltpu.get_barrier_semaphore()

    def greet(k, carry):
        pl.semaphore_signal(barrier, inc=1, device_id=peer(k)[1], device_id_type=MESH)
        return carry

    lax.fori_loop(1, chips, greet, 0)
    for dev in (partner, (row, z_up), (row, z_down)):
        pl.semaphore_signal(barrier, inc=1, device_id=dev, device_id_type=MESH)

    def gram_step(p, s):
        rs = pl.ds(pl.multiple_of(s * step_rows, step_rows), step_rows)
        lead, mate = xv[2 * p, rs, :], xv[2 * p + 1, rs, :]
        lh, ll = split(lead)
        mh, ml = split(mate)
        gram[p] += mm_t(lh, mh) + (mm_t(lh, ml) + mm_t(ll, mh))
        sq[p, 0] += jnp.sum((lead * lead).reshape(step_rows // 8, 8, BLK), axis=0)
        sq[p, 1] += jnp.sum((mate * mate).reshape(step_rows // 8, 8, BLK), axis=0)

    def squares(p):
        lead_sq = jnp.sum(sq[p, 0], axis=0, keepdims=True)
        mate_sq = jnp.sum(sq[p, 1], axis=0, keepdims=True)
        return jnp.concatenate(
            [lead_sq[:, :HALF], lead_sq[:, HALF:], mate_sq[:, :HALF], mate_sq[:, HALF:], jnp.zeros((4, HALF), f32)],
            axis=0,
        )

    def part_copy(rnd):
        return pltpu.make_async_remote_copy(
            part_send.at[rnd], part_recv.at[rnd], part_s.at[rnd], part_r.at[rnd], device_id=partner, device_id_type=MESH
        )

    def send_part(rnd):
        part_send[rnd, 0:BLK, :] = gram[other, :, 0:HALF]
        part_send[rnd, BLK : 2 * BLK, :] = gram[other, :, HALF:BLK]
        part_send[rnd, 2 * BLK : 2 * BLK + 8, :] = squares(other)
        part_copy(rnd).start()

    def reduce_gram(rnd):
        own_sq = squares(core)
        part_copy(rnd).wait()
        left = gram[core, :, 0:HALF] + part_recv[rnd, 0:BLK, :]
        right = gram[core, :, HALF:BLK] + part_recv[rnd, BLK : 2 * BLK, :]
        both_sq = own_sq + part_recv[rnd, 2 * BLK : 2 * BLK + 8, :]
        rs_src[rnd, :, 0:crow, :] = left.reshape(chips, crow, HALF)
        rs_src[rnd, :, crow : 2 * crow, :] = right.reshape(chips, crow, HALF)
        rs_src[rnd, :, 2 * crow : 2 * crow + 8, :] = jnp.broadcast_to(both_sq[None], (chips, 8, HALF))

        def rs_copy(k):
            t, dev = peer(k)
            return pltpu.make_async_remote_copy(
                rs_src.at[rnd, t], rs_recv.at[rnd, chip], rs_s.at[rnd, k], rs_r.at[rnd, chip],
                device_id=dev, device_id_type=MESH,
            )

        def ag_copy(k):
            _, dev = peer(k)
            return pltpu.make_async_remote_copy(
                ag.at[rnd, chip], ag.at[rnd, chip], ag_s.at[rnd, k], ag_r.at[rnd, chip],
                device_id=dev, device_id_type=MESH,
            )

        def rs_arrival(t):
            return pltpu.make_async_remote_copy(
                rs_src.at[rnd, t], rs_recv.at[rnd, t], rs_s.at[rnd, 0], rs_r.at[rnd, t],
                device_id=partner, device_id_type=MESH,
            )

        def ag_arrival(t):
            return pltpu.make_async_remote_copy(
                ag.at[rnd, t], ag.at[rnd, t], ag_s.at[rnd, 0], ag_r.at[rnd, t],
                device_id=partner, device_id_type=MESH,
            )

        def each(fn):
            def step(k, carry):
                fn(k)
                return carry

            lax.fori_loop(1, chips, step, 0)

        each(lambda k: rs_copy(k).start())
        rs_recv[rnd, chip] = rs_src[rnd, chip]
        each(lambda k: rs_arrival(peer(k)[0]).wait_recv())
        total = jnp.sum(rs_recv[rnd], axis=0)
        ag[rnd, chip] = total[0 : 2 * crow]
        each(lambda k: ag_copy(k).start())
        each(lambda k: rs_copy(k).wait_send())
        each(lambda k: ag_arrival(peer(k)[0]).wait_recv())
        each(lambda k: ag_copy(k).wait_send())
        return total[2 * crow : 2 * crow + 8]

    def rotation(rnd, sums):
        lead_sq = jnp.concatenate([sums[0:1], sums[1:2]], axis=1)
        mate_sq = jnp.concatenate([sums[2:3], sums[3:4]], axis=1)
        lead_col = jnp.broadcast_to(lead_sq, (8, BLK)).T[:, 0:1]
        cross = jnp.concatenate(
            [ag[rnd, :, 0:crow, :].reshape(BLK, HALF), ag[rnd, :, crow : 2 * crow, :].reshape(BLK, HALF)], axis=1
        )
        cmat[...] = cross / (lead_col + mate_sq + EPS)
        ident = eye()
        gmat[...] = ident + 0.25 * full(cmat[...], cmat[...], ((1,), (1,)))
        scale = 2.0 / (1.0 + BOUND)
        rx[0:BLK] = ident - scale * gmat[...]
        rx[BLK : 2 * BLK] = scale * ident

        def step(_, radius):
            s = 2.0 / (2.0 - radius * radius)
            hi, lo = split(rx[...])
            prod = mm3((hi, lo), (hi[0:BLK], lo[0:BLK]))
            rx[0:BLK] = s * prod[0:BLK] + (1.0 - s) * eye()
            rx[BLK : 2 * BLK] = s * (rx[BLK : 2 * BLK] + prod[BLK : 2 * BLK])
            return radius * radius / (2.0 - radius * radius)

        lax.fori_loop(0, STEPS, step, f32((BOUND - 1.0) / (BOUND + 1.0)))

        def correct(_, carry):
            x = rx[BLK : 2 * BLK]
            err = eye() - full(gmat[...], x, ((1,), (0,)))
            rx[BLK : 2 * BLK] = x + mm3(split(x), split(err))
            return carry

        lax.fori_loop(0, 2, correct, 0)
        inv = rx[BLK : 2 * BLK]
        w = full(inv, cmat[...], ((1,), (0,)))
        qv[rnd, core, 0] = 2.0 * inv - ident
        qv[rnd, core, 1] = w
        qv[rnd, core, 2] = ident - 0.5 * full(cmat[...], w, ((0,), (0,)))

    def q_copy(rnd, p):
        return pltpu.make_async_remote_copy(
            qv.at[rnd, p], qv.at[rnd, p], q_s.at[rnd], q_r.at[rnd], device_id=partner, device_id_type=MESH
        )

    def rotate(p, s):
        rs = pl.ds(pl.multiple_of(s * step_rows, step_rows), step_rows)
        x = jnp.concatenate([xv[2 * p, rs, :], xv[2 * p + 1, rs, :]], axis=1)
        xh, xl = split(x)
        for h in range(2):
            cols = slice(h * BLK, (h + 1) * BLK)
            nv[2 * p + h, rs, :] = mm3((xh, xl), (qhi[p, :, cols], qlo[p, :, cols]))

    def loop(n, fn):
        def step(s, carry):
            fn(s)
            return carry

        lax.fori_loop(0, n, step, 0)

    up_slot = down_slot = jnp.int32(0)
    for j in range(4):
        above, below = plan_ref[1, z_up * 4 + j], plan_ref[1, z_down * 4 + j]
        up_slot = jnp.where(above // 4 == z, above - 4 * z, up_slot)
        down_slot = jnp.where(below // 4 == z, below - 4 * z, down_slot)
    origin = [plan_ref[1, z * 4 + j] for j in range(4)]

    def z_copy(way, s):
        rs = pl.ds(s * step_rows, step_rows)
        return pltpu.make_async_remote_copy(
            zsend.at[way, rs, :], zrecv.at[way, rs, :], z_s.at[way, s], z_r.at[way, s],
            device_id=(row, z_up if way == 0 else z_down), device_id_type=MESH,
        )

    gram[...] = jnp.zeros_like(gram)
    sq[...] = jnp.zeros_like(sq)
    loads[0].wait()
    loads[1].wait()
    loop(n_steps, lambda s: gram_step(other, s))
    pl.semaphore_wait(barrier, chips + 2)
    send_part(0)
    loads[2].wait()
    loads[3].wait()
    loop(n_steps, lambda s: gram_step(core, s))
    rotation(0, reduce_gram(0))
    q_copy(0, core).start()
    put_rotation([qv[0, core, i] for i in range(3)], qhi, qlo, core)
    loop(n_steps, lambda s: rotate(core, s))
    q_copy(0, core).wait_send()
    q_copy(0, other).wait_recv()
    put_rotation([qv[0, other, i] for i in range(3)], qhi, qlo, other)
    for s in range(n_steps):
        rotate(other, s)
        rs = pl.ds(s * step_rows, step_rows)
        zsend[0, rs, :] = nv[up_slot, rs, :]
        z_copy(0, s).start()
        zsend[1, rs, :] = nv[down_slot, rs, :]
        z_copy(1, s).start()

    gram[...] = jnp.zeros_like(gram)
    sq[...] = jnp.zeros_like(sq)
    outs = []
    for s in range(n_steps):
        rs = pl.ds(s * step_rows, step_rows)
        z_copy(0, s).wait_recv()
        z_copy(1, s).wait_recv()
        for j in range(4):
            home = origin[j] // 4
            own = nv[jnp.clip(origin[j] - 4 * z, 0, 3), rs, :]
            xv[j, rs, :] = jnp.where(
                home == z, own, jnp.where(home < z, zrecv[0, rs, :], zrecv[1, rs, :])
            )
            outs.append(
                pltpu.make_async_copy(xv.at[j, rs, :], x2_ref.at[rs, j * BLK : (j + 1) * BLK], out_sem.at[s, j])
            )
            outs[-1].start()
        gram_step(other, s)
        if s == n_steps - 1:
            send_part(1)
        gram_step(core, s)
    for s in range(n_steps):
        z_copy(0, s).wait_send()
        z_copy(1, s).wait_send()
    rotation(1, reduce_gram(1))
    q_copy(1, core).start()
    for copy in outs:
        copy.wait()
    q_copy(1, core).wait_send()
    q_copy(1, other).wait_recv()
    final = pltpu.make_async_copy(qv.at[1], q_ref, load_sem.at[0])
    final.start()
    final.wait()


def two_rounds(plan, x, n_row, n_col):
    rows = x.shape[0]
    step_rows = rows // 4
    chips = n_row // 2
    crow = BLK // chips
    dma = pltpu.SemaphoreType.DMA
    return pl.pallas_call(
        functools.partial(rounds_kernel, n_row, n_col, rows, step_rows),
        out_shape=[jax.ShapeDtypeStruct(x.shape, f32), jax.ShapeDtypeStruct((2, 3, BLK, BLK), f32)],
        in_specs=[pl.BlockSpec(memory_space=pltpu.SMEM), pl.BlockSpec(memory_space=pl.ANY)],
        out_specs=[pl.BlockSpec(memory_space=pl.ANY)] * 2,
        scratch_shapes=[
            pltpu.VMEM((4, rows, BLK), f32),
            pltpu.VMEM((4, rows, BLK), f32),
            pltpu.VMEM((2, rows, BLK), f32),
            pltpu.VMEM((2, rows, BLK), f32),
            pltpu.VMEM((2, BLK, BLK), f32),
            pltpu.VMEM((2, 2, 8, BLK), f32),
            pltpu.VMEM((2, 2 * BLK + 8, HALF), f32),
            pltpu.VMEM((2, 2 * BLK + 8, HALF), f32),
            pltpu.VMEM((2, chips, 2 * crow + 8, HALF), f32),
            pltpu.VMEM((2, chips, 2 * crow + 8, HALF), f32),
            pltpu.VMEM((2, chips, 2 * crow, HALF), f32),
            pltpu.VMEM((2 * BLK, BLK), f32),
            pltpu.VMEM((BLK, BLK), f32),
            pltpu.VMEM((BLK, BLK), f32),
            pltpu.VMEM((2, 2, 3, BLK, BLK), f32),
            pltpu.VMEM((2, 2 * BLK, 2 * BLK), bf16),
            pltpu.VMEM((2, 2 * BLK, 2 * BLK), bf16),
            dma((4,)),
            dma((2,)), dma((2,)),
            dma((2, chips)), dma((2, chips)),
            dma((2, chips)), dma((2, chips)),
            dma((2,)), dma((2,)),
            dma((2, 4)), dma((2, 4)),
            dma((4, 4)),
        ],
        compiler_params=pltpu.CompilerParams(collective_id=0, has_side_effects=True, vmem_limit_bytes=56 << 20),
    )(plan, x)


def rotate_kernel(x_ref, q_ref, o_ref, qhi, qlo):
    @pl.when(pl.program_id(0) == 0)
    def _():
        for p in range(2):
            put_rotation([q_ref[p, i] for i in range(3)], qhi, qlo, p)

    for p in range(2):
        xh, xl = split(x_ref[:, 2 * p * BLK : (2 * p + 2) * BLK])
        for h in range(2):
            cols = slice(h * BLK, (h + 1) * BLK)
            o_ref[:, (2 * p + h) * BLK : (2 * p + h + 1) * BLK] = mm3(
                (xh, xl), (qhi[p, :, cols], qlo[p, :, cols])
            )


def last_rotation(x, q):
    rows = x.shape[0]
    step_rows = rows // 4
    return pl.pallas_call(
        rotate_kernel,
        grid=(rows // step_rows,),
        out_shape=jax.ShapeDtypeStruct(x.shape, f32),
        in_specs=[
            pl.BlockSpec((step_rows, 4 * BLK), lambda i: (i, 0)),
            pl.BlockSpec((2, 3, BLK, BLK), lambda i: (0, 0, 0, 0)),
        ],
        out_specs=pl.BlockSpec((step_rows, 4 * BLK), lambda i: (i, 0)),
        scratch_shapes=[pltpu.VMEM((2, 2 * BLK, 2 * BLK), bf16)] * 2,
        compiler_params=pltpu.CompilerParams(vmem_limit_bytes=48 << 20),
    )(x, q)


def shards(n_row, n_col, activations, plan):
    x2, q = two_rounds(plan, activations, n_row, n_col)
    return last_rotation(x2, q)


def solution(mesh):
    placed = (P("row", "col"), P())
    return jax.shard_map(
        functools.partial(shards, mesh.shape["row"], mesh.shape["col"]),
        mesh=mesh, in_specs=placed, out_specs=P("row", "col"), check_vma=False,
    )
```

time: 837 us -> 98 us (0.12)
  other arithmetic: 455 us -> 0 us
  blocking collectives: 130 us -> 0 us
  waiting for transfers between devices: 107 us -> 0 us
  Pallas kernels: 0 us -> 94.2 us
  matrix products: 61.1 us -> 0 us
  local copies, waits for them, and re-layouts: 60 us -> 3.59 us
  between operations: 14.6 us -> 0.02 us
    another operation x39 -> x0, other arithmetic: 439 us -> none  [the longest x30 274 us: inverse_spd(): factor = jnp.linalg.cholesky(matrix)]
    psum x2 -> x0, blocking collectives: 130 us -> none  [shards(): lax.psum((cross_gram, lead_sq, mate_sq), 'row')]
    pallas_call x0 -> x2, Pallas kernels: none -> 94.2 us  [the longest x1 88.9 us: two_rounds(): pl.pallas_call(functools.partial(rounds_kernel, n_row, n_col, rows, step_...]
    psum x2 -> x0, waiting for transfers between devices: 88.2 us -> none  [shards(): lax.psum((cross_gram, lead_sq, mate_sq), 'row')]
    dot_general x18 -> x0, matrix products: 45.7 us -> none  [the longest x2 9.44 us: local_sums(): jnp.einsum('rpa,rpb->pab', lead_block, mate_block, precision=highest)]
    another operation x40 -> x0, local copies, waits for them, and re-layouts: 28.3 us -> none  [the longest x30 19.3 us: inverse_spd(): jax.scipy.linalg.solve_triangular(factor, unit_batch, lower=True)]
    ppermute x2 -> x0, waiting for transfers between devices: 18.6 us -> none  [shifted(): return lax.ppermute(value, axis, pairs)]
    another operation x20 -> x0, matrix products: 15.4 us -> none  [the longest x12 8.44 us: inverse_spd(): jax.scipy.linalg.solve_triangular(factor, unit_batch, lower=True)]
  transfers between devices with their start and end apart: 4 -> 0, of which waited for: 4 -> 0; matrix products, arithmetic and copies ran while one was open for 2% -> 0% of each run, Pallas kernels for 0% -> 0%
where the time goes in v1:
time: 98 us; the launch traced here: 97.8 us
  Pallas kernels  94.2 us (96%)
  local copies, waits for them, and re-layouts  3.59 us (4%)
    pallas_call x1, Pallas kernels, two_rounds(): pl.pallas_call(functools.partial(rounds_kernel, n_row, n_col, rows, step_...  88.9 us
    pallas_call x1, Pallas kernels, last_rotation(): pl.pallas_call(rotate_kernel, grid=(rows // step_rows,), out_shape=jax.Sh...  5.35 us
    unnamed x4, local copies, waits for them, and re-layouts  3.59 us

profile of v1, /device:TPU:1, one launch (start us, length us, event | category | flops | bytes accessed | tf_op | source)
XLA Modules:
  0.0 97.8 jit_solution(9988885820116851997)
XLA Ops:
  0.0 88.9 %shard_map.28 = (f32[1024,1024]{1,0:T(8,128)}, f32[2,3,256,256]{3,2,1,0:T(8,128)}) custom-call(s32[2,32]{1,0:T(2,128)} %plan_ref.1, f32[1024,1024]{1,0:T(8,128)} %x_ref.1), custom_call_target="tpu_custom_call" | custom-call | tf_op jit(solution)/shard_map/pallas_call | solution.py:310
  88.9 0.0 copy-start
  88.9 2.2 %copy-done = f32[1024,1024]{1,0:T(8,128)S(1)} copy-done((f32[1024,1024]{1,0:T(8,128)S(1)}, f32[1024,1024]{1,0:T(8,128)}, u32[]{:S(2)}) %copy-start) | copy-done | bytes 4194328
  91.1 0.0 copy-start.1
  91.1 1.4 %copy-done.1 = f32[2,3,256,256]{3,2,1,0:T(8,128)S(1)} copy-done((f32[2,3,256,256]{3,2,1,0:T(8,128)S(1)}, f32[2,3,256,256]{3,2,1,0:T(8,128)}, u32[]{:S(2)}) %copy-start.1) | copy-done | bytes 1572888
  92.5 5.3 %shard_map.29 = f32[1024,1024]{1,0:T(8,128)} custom-call(f32[1024,1024]{1,0:T(8,128)S(1)} %copy-done, f32[2,3,256,256]{3,2,1,0:T(8,128)S(1)} %copy-done.1), custom_call_target="tpu_custom_call" | custom-call | tf_op jit(solution)/shard_map/pallas_call | solution.py:363
Async XLA Ops:
  88.9 2.2 %copy-start = (f32[1024,1024]{1,0:T(8,128)S(1)}, f32[1024,1024]{1,0:T(8,128)}, u32[]{:S(2)}) copy-start(f32[1024,1024]{1,0:T(8,128)} %get-tuple-element.7.x_ref) | copy-start | bytes 12582916
  91.1 1.4 %copy-start.1 = (f32[2,3,256,256]{3,2,1,0:T(8,128)S(1)}, f32[2,3,256,256]{3,2,1,0:T(8,128)}, u32[]{:S(2)}) copy-start(f32[2,3,256,256]{3,2,1,0:T(8,128)} %get-tuple-element.8.q_ref) | copy-start | bytes 4718596

commit v2 on v1

--- a/solution.py
+++ b/solution.py
@@ -1,4 +1,5 @@
 import functools
+import math
 
 import jax
 import jax.numpy as jnp
@@ -10,7 +11,7 @@
 BLK = 256
 HALF = 128
 EPS = 1e-6
-STEPS = 9
+STEPS = 7
 BOUND = 1.02 * (1.0 + (BLK / 2) ** 2 / 4)
 MESH = pl.DeviceIdType.MESH
 HIGHEST = lax.Precision.HIGHEST
@@ -55,7 +56,7 @@
 def rounds_kernel(
     n_row, n_col, rows, step_rows,
     plan_ref, x_ref, x2_ref, q_ref,
-    xv, nv, zsend, zrecv, gram, sq, part_send, part_recv, rs_src, rs_recv, ag, rx, gmat, cmat, qv, qhi, qlo,
+    xv, nv, zsend, zrecv, gram, sq, part_send, part_recv, rs_src, rs_recv, ag, gmat, cmat, qv, qhi, qlo,
     load_sem, part_s, part_r, rs_s, rs_r, ag_s, ag_r, q_s, q_r, z_s, z_r, out_sem,
 ):
     chips = n_row // 2
@@ -67,9 +68,20 @@
     z_up, z_down = lax.rem(z + 1, n_col), lax.rem(z + n_col - 1, n_col)
     n_steps = rows // step_rows
 
-    def peer(k):
-        t = lax.rem(chip + k, chips)
-        return t, (t * 2 + core, z)
+    side = math.isqrt(chips)
+    cx, cy = chip // side, lax.rem(chip, side)
+
+    def hops(offset):
+        return min(offset, side - offset)
+
+    far_first = sorted(
+        [(dx, dy) for dx in range(side) for dy in range(side) if (dx, dy) != (0, 0)],
+        key=lambda d: -hops(d[0]) - hops(d[1]),
+    )
+    peers = []
+    for dx, dy in far_first:
+        t = lax.rem(cx + dx, side) * side + lax.rem(cy + dy, side)
+        peers.append((t, (t * 2 + core, z)))
 
     loads = []
     for i, p in enumerate((other, core)):
@@ -80,12 +92,7 @@
 
     barrier = pltpu.get_barrier_semaphore()
 
-    def greet(k, carry):
-        pl.semaphore_signal(barrier, inc=1, device_id=peer(k)[1], device_id_type=MESH)
-        return carry
-
-    lax.fori_loop(1, chips, greet, 0)
-    for dev in (partner, (row, z_up), (row, z_down)):
+    for dev in [dev for _, dev in peers] + [(row, z_up), (row, z_down), partner]:
         pl.semaphore_signal(barrier, inc=1, device_id=dev, device_id_type=MESH)
 
     def gram_step(p, s):
@@ -126,48 +133,35 @@
         rs_src[rnd, :, crow : 2 * crow, :] = right.reshape(chips, crow, HALF)
         rs_src[rnd, :, 2 * crow : 2 * crow + 8, :] = jnp.broadcast_to(both_sq[None], (chips, 8, HALF))
 
-        def rs_copy(k):
-            t, dev = peer(k)
+        sent = crow * 2 + 4
+
+        def rs_copy(k, t, dev, source):
             return pltpu.make_async_remote_copy(
-                rs_src.at[rnd, t], rs_recv.at[rnd, chip], rs_s.at[rnd, k], rs_r.at[rnd, chip],
+                rs_src.at[rnd, t, 0:sent], rs_recv.at[rnd, source, 0:sent], rs_s.at[rnd, k], rs_r.at[rnd, source],
                 device_id=dev, device_id_type=MESH,
             )
 
-        def ag_copy(k):
-            _, dev = peer(k)
+        def ag_copy(k, dev, source):
             return pltpu.make_async_remote_copy(
-                ag.at[rnd, chip], ag.at[rnd, chip], ag_s.at[rnd, k], ag_r.at[rnd, chip],
+                ag.at[rnd, source], ag.at[rnd, source], ag_s.at[rnd, k], ag_r.at[rnd, source],
                 device_id=dev, device_id_type=MESH,
             )
 
-        def rs_arrival(t):
-            return pltpu.make_async_remote_copy(
-                rs_src.at[rnd, t], rs_recv.at[rnd, t], rs_s.at[rnd, 0], rs_r.at[rnd, t],
-                device_id=partner, device_id_type=MESH,
-            )
-
-        def ag_arrival(t):
-            return pltpu.make_async_remote_copy(
-                ag.at[rnd, t], ag.at[rnd, t], ag_s.at[rnd, 0], ag_r.at[rnd, t],
-                device_id=partner, device_id_type=MESH,
-            )
-
-        def each(fn):
-            def step(k, carry):
-                fn(k)
-                return carry
-
-            lax.fori_loop(1, chips, step, 0)
-
-        each(lambda k: rs_copy(k).start())
+        for k, (t, dev) in enumerate(peers):
+            rs_copy(k, t, dev, chip).start()
         rs_recv[rnd, chip] = rs_src[rnd, chip]
-        each(lambda k: rs_arrival(peer(k)[0]).wait_recv())
+        for k, (t, dev) in enumerate(peers):
+            rs_copy(k, t, dev, t).wait_recv()
         total = jnp.sum(rs_recv[rnd], axis=0)
         ag[rnd, chip] = total[0 : 2 * crow]
-        each(lambda k: ag_copy(k).start())
-        each(lambda k: rs_copy(k).wait_send())
-        each(lambda k: ag_arrival(peer(k)[0]).wait_recv())
-        each(lambda k: ag_copy(k).wait_send())
+        for k, (t, dev) in enumerate(peers):
+            ag_copy(k, dev, chip).start()
+        for k, (t, dev) in enumerate(peers):
+            rs_copy(k, t, dev, chip).wait_send()
+        for k, (t, dev) in enumerate(peers):
+            ag_copy(k, dev, t).wait_recv()
+        for k, (t, dev) in enumerate(peers):
+            ag_copy(k, dev, chip).wait_send()
         return total[2 * crow : 2 * crow + 8]
 
     def rotation(rnd, sums):
@@ -181,27 +175,23 @@
         ident = eye()
         gmat[...] = ident + 0.25 * full(cmat[...], cmat[...], ((1,), (1,)))
         scale = 2.0 / (1.0 + BOUND)
-        rx[0:BLK] = ident - scale * gmat[...]
-        rx[BLK : 2 * BLK] = scale * ident
-
-        def step(_, radius):
+        radius = (BOUND - 1.0) / (BOUND + 1.0)
+        res = split(ident - scale * gmat[...])
+        inv = None
+        for k in range(STEPS):
             s = 2.0 / (2.0 - radius * radius)
-            hi, lo = split(rx[...])
-            prod = mm3((hi, lo), (hi[0:BLK], lo[0:BLK]))
-            rx[0:BLK] = s * prod[0:BLK] + (1.0 - s) * eye()
-            rx[BLK : 2 * BLK] = s * (rx[BLK : 2 * BLK] + prod[BLK : 2 * BLK])
-            return radius * radius / (2.0 - radius * radius)
-
-        lax.fori_loop(0, STEPS, step, f32((BOUND - 1.0) / (BOUND + 1.0)))
-
-        def correct(_, carry):
-            x = rx[BLK : 2 * BLK]
-            err = eye() - full(gmat[...], x, ((1,), (0,)))
-            rx[BLK : 2 * BLK] = x + mm3(split(x), split(err))
-            return carry
-
-        lax.fori_loop(0, 2, correct, 0)
-        inv = rx[BLK : 2 * BLK]
+            radius = radius * radius / (2.0 - radius * radius)
+            if k < STEPS - 1:
+                square = mm3(res, res)
+            if k == 0:
+                inv = (s * scale) * (ident + (res[0].astype(f32) + res[1].astype(f32)))
+            else:
+                inv = s * (inv + mm3(split(inv), res))
+            if k < STEPS - 1:
+                res = split(s * square + (1.0 - s) * ident)
+        inv_parts = split(inv)
+        inv = inv + mm3(inv_parts, split(ident - mm3(split(gmat[...]), inv_parts)))
+        inv = inv + mm3(split(inv), split(ident - full(gmat[...], inv, ((1,), (0,)))))
         w = full(inv, cmat[...], ((1,), (0,)))
         qv[rnd, core, 0] = 2.0 * inv - ident
         qv[rnd, core, 1] = w
@@ -210,6 +200,11 @@
     def q_copy(rnd, p):
         return pltpu.make_async_remote_copy(
             qv.at[rnd, p], qv.at[rnd, p], q_s.at[rnd], q_r.at[rnd], device_id=partner, device_id_type=MESH
+        )
+
+    def q_out(p):
+        return pltpu.make_async_remote_copy(
+            qv.at[1, p], q_ref.at[p], q_s.at[1], q_r.at[1], device_id=partner, device_id_type=MESH
         )
 
     def rotate(p, s):
@@ -291,14 +286,14 @@
         z_copy(0, s).wait_send()
         z_copy(1, s).wait_send()
     rotation(1, reduce_gram(1))
-    q_copy(1, core).start()
+    q_out(core).start()
+    final = pltpu.make_async_copy(qv.at[1, core], q_ref.at[core], load_sem.at[0])
+    final.start()
     for copy in outs:
         copy.wait()
-    q_copy(1, core).wait_send()
-    q_copy(1, other).wait_recv()
-    final = pltpu.make_async_copy(qv.at[1], q_ref, load_sem.at[0])
-    final.start()
     final.wait()
+    q_out(core).wait_send()
+    q_out(other).wait_recv()
 
 
 def two_rounds(plan, x, n_row, n_col):
@@ -324,7 +319,6 @@
             pltpu.VMEM((2, chips, 2 * crow + 8, HALF), f32),
             pltpu.VMEM((2, chips, 2 * crow + 8, HALF), f32),
             pltpu.VMEM((2, chips, 2 * crow, HALF), f32),
-            pltpu.VMEM((2 * BLK, BLK), f32),
             pltpu.VMEM((BLK, BLK), f32),
             pltpu.VMEM((BLK, BLK), f32),
             pltpu.VMEM((2, 2, 3, BLK, BLK), f32),
@@ -370,7 +364,7 @@
         ],
         out_specs=pl.BlockSpec((step_rows, 4 * BLK), lambda i: (i, 0)),
         scratch_shapes=[pltpu.VMEM((2, 2 * BLK, 2 * BLK), bf16)] * 2,
-        compiler_params=pltpu.CompilerParams(vmem_limit_bytes=48 << 20),
+        compiler_params=pltpu.CompilerParams(vmem_limit_bytes=60 << 20),
     )(x, q)
 
 

time: 98 us -> 90.1 us (0.919)
  Pallas kernels: 94.2 us -> 90 us
  local copies, waits for them, and re-layouts: 3.59 us -> 0 us
    pallas_call x1, Pallas kernels: 88.9 us -> 82.2 us  [two_rounds(): pl.pallas_call(functools.partial(rounds_kernel, n_row, n_col, rows, step_...]
    unnamed x4 -> x0, local copies, waits for them, and re-layouts: 3.59 us -> none
    pallas_call x1, Pallas kernels: 5.35 us -> 7.79 us  [last_rotation(): pl.pallas_call(rotate_kernel, grid=(rows // step_rows,), out_shape=jax.Sh...]
where the time goes in v2:
time: 90.1 us; the launch traced here: 90 us
  Pallas kernels  90 us (100%)
    pallas_call x1, Pallas kernels, two_rounds(): pl.pallas_call(functools.partial(rounds_kernel, n_row, n_col, rows, step_...  82.2 us
    pallas_call x1, Pallas kernels, last_rotation(): pl.pallas_call(rotate_kernel, grid=(rows // step_rows,), out_shape=jax.Sh...  7.79 us

profile of v2, /device:TPU:1, one launch (start us, length us, event | category | flops | bytes accessed | tf_op | source)
XLA Modules:
  0.0 90.0 jit_solution(15712541320158201846)
XLA Ops:
  0.0 82.2 %shard_map.28 = (f32[1024,1024]{1,0:T(8,128)}, f32[2,3,256,256]{3,2,1,0:T(8,128)}) custom-call(s32[2,32]{1,0:T(2,128)} %plan_ref.1, f32[1024,1024]{1,0:T(8,128)} %x_ref.1), custom_call_target="tpu_custom_call" | custom-call | tf_op jit(solution)/shard_map/pallas_call | solution.py:305
  82.2 7.8 %shard_map.29 = f32[1024,1024]{1,0:T(8,128)} custom-call(f32[1024,1024]{1,0:T(8,128)} %get-tuple-element.7.x_ref, f32[2,3,256,256]{3,2,1,0:T(8,128)} %get-tuple-element.8.q_ref), custom_call_target="tpu_custom_call" | custom-call | tf_op jit(solution)/shard_map/pallas_call | solution.py:357

commit v3 on v2

--- a/solution.py
+++ b/solution.py
@@ -45,19 +45,23 @@
     return jnp.where(rows == cols, 1.0, 0.0).astype(f32)
 
 
-def put_rotation(q, hi_ref, lo_ref, pair):
+def put_rotation(q, hi_ref, lo_ref, pair, whole_ref=None):
     q11, w, q22 = q
     for value, r, c in ((q11, 0, 0), (w, 0, 1), (-w.T, 1, 0), (q22, 1, 1)):
         hi, lo = split(value)
         hi_ref[pair, r * BLK : (r + 1) * BLK, c * BLK : (c + 1) * BLK] = hi
         lo_ref[pair, r * BLK : (r + 1) * BLK, c * BLK : (c + 1) * BLK] = lo
+        if whole_ref is not None:
+            whole_ref[2 * pair + c, r] = value
 
 
 def rounds_kernel(
-    n_row, n_col, rows, step_rows,
+    n_row, n_col, rows,
     plan_ref, x_ref, x2_ref, q_ref,
-    xv, nv, zsend, zrecv, gram, sq, part_send, part_recv, rs_src, rs_recv, ag, gmat, cmat, qv, qhi, qlo,
+    xv, nv, zsend, zrecv, gram, sq, part_send, part_recv, rs_src, rs_recv, ag, gmat, cmat, qv, qhi, qlo, qf,
+    esend, erecv, zearly, qz, qz_all, qz_other,
     load_sem, part_s, part_r, rs_s, rs_r, ag_s, ag_r, q_s, q_r, z_s, z_r, out_sem,
+    e_s, e_r, qz_s, qz_r, qa_s, qa_r, qp_s, qp_r,
 ):
     chips = n_row // 2
     crow = BLK // chips
@@ -66,7 +70,9 @@
     other = 1 - core
     partner = (chip * 2 + other, z)
     z_up, z_down = lax.rem(z + 1, n_col), lax.rem(z + n_col - 1, n_col)
-    n_steps = rows // step_rows
+    unit = rows // 8
+    late = [(0, 2 * unit), (2 * unit, 2 * unit), (4 * unit, unit)]
+    early, n_early = 5 * unit, 3 * unit
 
     side = math.isqrt(chips)
     cx, cy = chip // side, lax.rem(chip, side)
@@ -95,8 +101,8 @@
     for dev in [dev for _, dev in peers] + [(row, z_up), (row, z_down), partner]:
         pl.semaphore_signal(barrier, inc=1, device_id=dev, device_id_type=MESH)
 
-    def gram_step(p, s):
-        rs = pl.ds(pl.multiple_of(s * step_rows, step_rows), step_rows)
+    def gram_step(p, start, step_rows):
+        rs = pl.ds(start, step_rows)
         lead, mate = xv[2 * p, rs, :], xv[2 * p + 1, rs, :]
         lh, ll = split(lead)
         mh, ml = split(mate)
@@ -207,20 +213,13 @@
             qv.at[1, p], q_ref.at[p], q_s.at[1], q_r.at[1], device_id=partner, device_id_type=MESH
         )
 
-    def rotate(p, s):
-        rs = pl.ds(pl.multiple_of(s * step_rows, step_rows), step_rows)
+    def rotate(p, start, step_rows):
+        rs = pl.ds(start, step_rows)
         x = jnp.concatenate([xv[2 * p, rs, :], xv[2 * p + 1, rs, :]], axis=1)
         xh, xl = split(x)
         for h in range(2):
             cols = slice(h * BLK, (h + 1) * BLK)
             nv[2 * p + h, rs, :] = mm3((xh, xl), (qhi[p, :, cols], qlo[p, :, cols]))
-
-    def loop(n, fn):
-        def step(s, carry):
-            fn(s)
-            return carry
-
-        lax.fori_loop(0, n, step, 0)
 
     up_slot = down_slot = jnp.int32(0)
     for j in range(4):
@@ -229,62 +228,132 @@
         down_slot = jnp.where(below // 4 == z, below - 4 * z, down_slot)
     origin = [plan_ref[1, z * 4 + j] for j in range(4)]
 
-    def z_copy(way, s):
-        rs = pl.ds(s * step_rows, step_rows)
-        return pltpu.make_async_remote_copy(
-            zsend.at[way, rs, :], zrecv.at[way, rs, :], z_s.at[way, s], z_r.at[way, s],
+    def z_copy(way, i):
+        rs = pl.ds(*late[i])
+        return pltpu.make_async_remote_copy(
+            zsend.at[way, rs, :], zrecv.at[way, rs, :], z_s.at[way, i], z_r.at[way, i],
             device_id=(row, z_up if way == 0 else z_down), device_id_type=MESH,
+        )
+
+    def early_copy(way):
+        return pltpu.make_async_remote_copy(
+            esend.at[way], erecv.at[way], e_s.at[way], e_r.at[way],
+            device_id=(row, z_up if way == 0 else z_down), device_id_type=MESH,
+        )
+
+    def share_copy(way):
+        return pltpu.make_async_remote_copy(
+            qz.at[way], qz_all.at[chip, way], qz_s.at[way], qz_r.at[way],
+            device_id=(row, z_up if way == 0 else z_down), device_id_type=MESH,
+        )
+
+    def share_gather(k, dev, source):
+        return pltpu.make_async_remote_copy(
+            qz_all.at[source], qz_all.at[source], qa_s.at[k], qa_r.at[source], device_id=dev, device_id_type=MESH
+        )
+
+    def share_swap():
+        return pltpu.make_async_remote_copy(
+            qz_all, qz_other, qp_s.at[0], qp_r.at[0], device_id=partner, device_id_type=MESH
         )
 
     gram[...] = jnp.zeros_like(gram)
     sq[...] = jnp.zeros_like(sq)
     loads[0].wait()
     loads[1].wait()
-    loop(n_steps, lambda s: gram_step(other, s))
+    for start in range(0, rows, 2 * unit):
+        gram_step(other, start, 2 * unit)
+    loads[2].wait()
+    loads[3].wait()
     pl.semaphore_wait(barrier, chips + 2)
     send_part(0)
-    loads[2].wait()
-    loads[3].wait()
-    loop(n_steps, lambda s: gram_step(core, s))
+    for way, slot in enumerate((up_slot, down_slot)):
+        for h in range(2):
+            esend[way, h] = xv[(slot // 2) * 2 + h, pl.ds(early, n_early), :]
+        early_copy(way).start()
+    for start in range(0, rows, 2 * unit):
+        gram_step(core, start, 2 * unit)
     rotation(0, reduce_gram(0))
     q_copy(0, core).start()
-    put_rotation([qv[0, core, i] for i in range(3)], qhi, qlo, core)
-    loop(n_steps, lambda s: rotate(core, s))
+    put_rotation([qv[0, core, i] for i in range(3)], qhi, qlo, core, qf)
+    for start, size in late:
+        rotate(core, start, size)
     q_copy(0, core).wait_send()
     q_copy(0, other).wait_recv()
-    put_rotation([qv[0, other, i] for i in range(3)], qhi, qlo, other)
-    for s in range(n_steps):
-        rotate(other, s)
-        rs = pl.ds(s * step_rows, step_rows)
+    put_rotation([qv[0, other, i] for i in range(3)], qhi, qlo, other, qf)
+    for way, slot in enumerate((up_slot, down_slot)):
+        qz[way] = qf[slot, core, pl.ds(pl.multiple_of(chip * crow, crow), crow), :]
+        share_copy(way).start()
+    for i, (start, size) in enumerate(late):
+        rotate(other, start, size)
+        rs = pl.ds(start, size)
         zsend[0, rs, :] = nv[up_slot, rs, :]
-        z_copy(0, s).start()
+        z_copy(0, i).start()
         zsend[1, rs, :] = nv[down_slot, rs, :]
-        z_copy(1, s).start()
+        z_copy(1, i).start()
+    for way in range(2):
+        share_copy(way).wait_recv()
+    for k, (_, dev) in enumerate(peers):
+        share_gather(k, dev, chip).start()
+    rotate(core, early, n_early)
+    rotate(other, early, n_early)
 
     gram[...] = jnp.zeros_like(gram)
     sq[...] = jnp.zeros_like(sq)
     outs = []
-    for s in range(n_steps):
-        rs = pl.ds(s * step_rows, step_rows)
-        z_copy(0, s).wait_recv()
-        z_copy(1, s).wait_recv()
+
+    def place(start, size, lower, upper):
+        rs = pl.ds(start, size)
         for j in range(4):
             home = origin[j] // 4
             own = nv[jnp.clip(origin[j] - 4 * z, 0, 3), rs, :]
-            xv[j, rs, :] = jnp.where(
-                home == z, own, jnp.where(home < z, zrecv[0, rs, :], zrecv[1, rs, :])
-            )
+            xv[j, rs, :] = jnp.where(home == z, own, jnp.where(home < z, lower[...], upper[...]))
             outs.append(
-                pltpu.make_async_copy(xv.at[j, rs, :], x2_ref.at[rs, j * BLK : (j + 1) * BLK], out_sem.at[s, j])
+                pltpu.make_async_copy(
+                    xv.at[j, rs, :], x2_ref.at[rs, j * BLK : (j + 1) * BLK], out_sem.at[len(outs)]
+                )
             )
             outs[-1].start()
-        gram_step(other, s)
-        if s == n_steps - 1:
-            send_part(1)
-        gram_step(core, s)
-    for s in range(n_steps):
-        z_copy(0, s).wait_send()
-        z_copy(1, s).wait_send()
+
+    def arrive(i):
+        z_copy(0, i).wait_recv()
+        z_copy(1, i).wait_recv()
+        rs = pl.ds(*late[i])
+        place(*late[i], zrecv.at[0, rs, :], zrecv.at[1, rs, :])
+
+    arrive(0)
+    gram_step(other, *late[0])
+    gram_step(core, *late[0])
+    for k, (t, dev) in enumerate(peers):
+        share_gather(k, dev, t).wait_recv()
+    share_swap().start()
+    for way in range(2):
+        early_copy(way).wait_recv()
+    for way in range(2):
+        part = qz_all[:, way].reshape(BLK, BLK)
+        zearly[way] = mm3(split(erecv[way, core]), split(part))
+    share_swap().wait_recv()
+    for way in range(2):
+        part = qz_other[:, way].reshape(BLK, BLK)
+        zearly[way] += mm3(split(erecv[way, other]), split(part))
+    place(early, n_early, zearly.at[0], zearly.at[1])
+    gram_step(other, early, n_early)
+    gram_step(core, early, n_early)
+    arrive(1)
+    gram_step(other, *late[1])
+    gram_step(core, *late[1])
+    arrive(2)
+    gram_step(other, *late[2])
+    send_part(1)
+    gram_step(core, *late[2])
+    for way in range(2):
+        for i in range(len(late)):
+            z_copy(way, i).wait_send()
+        early_copy(way).wait_send()
+        share_copy(way).wait_send()
+    for k, (_, dev) in enumerate(peers):
+        share_gather(k, dev, chip).wait_send()
+    share_swap().wait_send()
     rotation(1, reduce_gram(1))
     q_out(core).start()
     final = pltpu.make_async_copy(qv.at[1, core], q_ref.at[core], load_sem.at[0])
@@ -298,12 +367,12 @@
 
 def two_rounds(plan, x, n_row, n_col):
     rows = x.shape[0]
-    step_rows = rows // 4
+    n_early = 3 * rows // 8
     chips = n_row // 2
     crow = BLK // chips
     dma = pltpu.SemaphoreType.DMA
     return pl.pallas_call(
-        functools.partial(rounds_kernel, n_row, n_col, rows, step_rows),
+        functools.partial(rounds_kernel, n_row, n_col, rows),
         out_shape=[jax.ShapeDtypeStruct(x.shape, f32), jax.ShapeDtypeStruct((2, 3, BLK, BLK), f32)],
         in_specs=[pl.BlockSpec(memory_space=pltpu.SMEM), pl.BlockSpec(memory_space=pl.ANY)],
         out_specs=[pl.BlockSpec(memory_space=pl.ANY)] * 2,
@@ -324,13 +393,24 @@
             pltpu.VMEM((2, 2, 3, BLK, BLK), f32),
             pltpu.VMEM((2, 2 * BLK, 2 * BLK), bf16),
             pltpu.VMEM((2, 2 * BLK, 2 * BLK), bf16),
+            pltpu.VMEM((4, 2, BLK, BLK), f32),
+            pltpu.VMEM((2, 2, n_early, BLK), f32),
+            pltpu.VMEM((2, 2, n_early, BLK), f32),
+            pltpu.VMEM((2, n_early, BLK), f32),
+            pltpu.VMEM((2, crow, BLK), f32),
+            pltpu.VMEM((chips, 2, crow, BLK), f32),
+            pltpu.VMEM((chips, 2, crow, BLK), f32),
             dma((4,)),
             dma((2,)), dma((2,)),
             dma((2, chips)), dma((2, chips)),
             dma((2, chips)), dma((2, chips)),
             dma((2,)), dma((2,)),
-            dma((2, 4)), dma((2, 4)),
-            dma((4, 4)),
+            dma((2, 3)), dma((2, 3)),
+            dma((16,)),
+            dma((2,)), dma((2,)),
+            dma((2,)), dma((2,)),
+            dma((chips,)), dma((chips,)),
+            dma((1,)), dma((1,)),
         ],
         compiler_params=pltpu.CompilerParams(collective_id=0, has_side_effects=True, vmem_limit_bytes=56 << 20),
     )(plan, x)

time: 90.1 us -> 82.1 us (0.911)
  Pallas kernels: 90 us -> 82 us
    pallas_call x1, Pallas kernels: 82.2 us -> 74.2 us  [two_rounds(): pl.pallas_call(functools.partial(rounds_kernel, n_row, n_col, rows), out_...]
where the time goes in v3:
time: 82.1 us; the launch traced here: 82 us
  Pallas kernels  82 us (100%)
    pallas_call x1, Pallas kernels, two_rounds(): pl.pallas_call(functools.partial(rounds_kernel, n_row, n_col, rows), out_...  74.2 us
    pallas_call x1, Pallas kernels, last_rotation(): pl.pallas_call(rotate_kernel, grid=(rows // step_rows,), out_shape=jax.Sh...  7.79 us

profile of v3, /device:TPU:1, one launch (start us, length us, event | category | flops | bytes accessed | tf_op | source)
XLA Modules:
  0.0 82.0 jit_solution(3503912833318688552)
XLA Ops:
  0.0 74.2 %shard_map.28 = (f32[1024,1024]{1,0:T(8,128)}, f32[2,3,256,256]{3,2,1,0:T(8,128)}) custom-call(s32[2,32]{1,0:T(2,128)} %plan_ref.1, f32[1024,1024]{1,0:T(8,128)} %x_ref.1), custom_call_target="tpu_custom_call" | custom-call | tf_op jit(solution)/shard_map/pallas_call | solution.py:374
  74.2 7.8 %shard_map.29 = f32[1024,1024]{1,0:T(8,128)} custom-call(f32[1024,1024]{1,0:T(8,128)} %get-tuple-element.7.x_ref, f32[2,3,256,256]{3,2,1,0:T(8,128)} %get-tuple-element.8.q_ref), custom_call_target="tpu_custom_call" | custom-call | tf_op jit(solution)/shard_map/pallas_call | solution.py:437

commit v4 on v3

--- a/solution.py
+++ b/solution.py
@@ -412,18 +412,19 @@
             dma((chips,)), dma((chips,)),
             dma((1,)), dma((1,)),
         ],
-        compiler_params=pltpu.CompilerParams(collective_id=0, has_side_effects=True, vmem_limit_bytes=56 << 20),
+        compiler_params=pltpu.CompilerParams(collective_id=0, has_side_effects=True, vmem_limit_bytes=48 << 20),
     )(plan, x)
 
 
-def rotate_kernel(x_ref, q_ref, o_ref, qhi, qlo):
+def rotate_kernel(step_rows, x_ref, q_ref, o_ref, qhi, qlo):
     @pl.when(pl.program_id(0) == 0)
     def _():
         for p in range(2):
             put_rotation([q_ref[p, i] for i in range(3)], qhi, qlo, p)
 
+    rs = pl.ds(pl.multiple_of(pl.program_id(0) * step_rows, step_rows), step_rows)
     for p in range(2):
-        xh, xl = split(x_ref[:, 2 * p * BLK : (2 * p + 2) * BLK])
+        xh, xl = split(x_ref[rs, 2 * p * BLK : (2 * p + 2) * BLK])
         for h in range(2):
             cols = slice(h * BLK, (h + 1) * BLK)
             o_ref[:, (2 * p + h) * BLK : (2 * p + h + 1) * BLK] = mm3(
@@ -435,16 +436,13 @@
     rows = x.shape[0]
     step_rows = rows // 4
     return pl.pallas_call(
-        rotate_kernel,
+        functools.partial(rotate_kernel, step_rows),
         grid=(rows // step_rows,),
         out_shape=jax.ShapeDtypeStruct(x.shape, f32),
-        in_specs=[
-            pl.BlockSpec((step_rows, 4 * BLK), lambda i: (i, 0)),
-            pl.BlockSpec((2, 3, BLK, BLK), lambda i: (0, 0, 0, 0)),
-        ],
+        in_specs=[pl.BlockSpec(memory_space=pltpu.VMEM)] * 2,
         out_specs=pl.BlockSpec((step_rows, 4 * BLK), lambda i: (i, 0)),
         scratch_shapes=[pltpu.VMEM((2, 2 * BLK, 2 * BLK), bf16)] * 2,
-        compiler_params=pltpu.CompilerParams(vmem_limit_bytes=60 << 20),
+        compiler_params=pltpu.CompilerParams(vmem_limit_bytes=20 << 20),
     )(x, q)
 
 

time: 82.1 us -> 80.3 us (0.978)
  Pallas kernels: 82 us -> 79.5 us
    pallas_call x1, Pallas kernels: 7.79 us -> 5.52 us  [last_rotation(): pl.pallas_call(functools.partial(rotate_kernel, step_rows), grid=(rows //...]
where the time goes in v4:
time: 80.3 us; the launch traced here: 80.2 us
  Pallas kernels  79.5 us (99%)
    pallas_call x1, Pallas kernels, two_rounds(): pl.pallas_call(functools.partial(rounds_kernel, n_row, n_col, rows), out_...  74 us
    pallas_call x1, Pallas kernels, last_rotation(): pl.pallas_call(functools.partial(rotate_kernel, step_rows), grid=(rows //...  5.52 us

profile of v4, /device:TPU:1, one launch (start us, length us, event | category | flops | bytes accessed | tf_op | source)
XLA Modules:
  0.0 80.2 jit_solution(3312929538385954580)
XLA Ops:
  0.0 0.0 copy-start
  0.0 0.7 copy-done
  0.7 74.0 %shard_map.28 = (f32[1024,1024]{1,0:T(8,128)S(1)}, f32[2,3,256,256]{3,2,1,0:T(8,128)S(1)}) custom-call(s32[2,32]{1,0:T(2,128)S(1)} %copy-done, f32[1024,1024]{1,0:T(8,128)} %x_ref.1), custom_call_target="tpu_custom_call" | custom-call | tf_op jit(solution)/shard_map/pallas_call | solution.py:374
  74.6 5.5 %shard_map.29 = f32[1024,1024]{1,0:T(8,128)} custom-call(f32[1024,1024]{1,0:T(8,128)S(1)} %get-tuple-element.7.x_ref, f32[2,3,256,256]{3,2,1,0:T(8,128)S(1)} %get-tuple-element.8.q_ref), custom_call_target="tpu_custom_call" | custom-call | tf_op jit(solution)/shard_map/pallas_call | solution.py:438
Async XLA Ops:
  0.0 0.7 copy-start

commit v5 on v4

--- a/solution.py
+++ b/solution.py
@@ -57,10 +57,10 @@
 
 def rounds_kernel(
     n_row, n_col, rows,
-    plan_ref, x_ref, x2_ref, q_ref,
+    plan_ref, x_ref, xh_ref, xl_ref, qh_ref, ql_ref,
     xv, nv, zsend, zrecv, gram, sq, part_send, part_recv, rs_src, rs_recv, ag, gmat, cmat, qv, qhi, qlo, qf,
     esend, erecv, zearly, qz, qz_all, qz_other,
-    load_sem, part_s, part_r, rs_s, rs_r, ag_s, ag_r, q_s, q_r, z_s, z_r, out_sem,
+    load_sem, part_s, part_r, rs_s, rs_r, ag_s, ag_r, q_s, q_r, z_s, z_r,
     e_s, e_r, qz_s, qz_r, qa_s, qa_r, qp_s, qp_r,
 ):
     chips = n_row // 2
@@ -71,8 +71,8 @@
     partner = (chip * 2 + other, z)
     z_up, z_down = lax.rem(z + 1, n_col), lax.rem(z + n_col - 1, n_col)
     unit = rows // 8
-    late = [(0, 2 * unit), (2 * unit, 2 * unit), (4 * unit, unit)]
-    early, n_early = 5 * unit, 3 * unit
+    late = [(0, 2 * unit), (2 * unit, unit), (3 * unit, unit)]
+    early, n_early = 4 * unit, 4 * unit
 
     side = math.isqrt(chips)
     cx, cy = chip // side, lax.rem(chip, side)
@@ -101,11 +101,16 @@
     for dev in [dev for _, dev in peers] + [(row, z_up), (row, z_down), partner]:
         pl.semaphore_signal(barrier, inc=1, device_id=dev, device_id_type=MESH)
 
-    def gram_step(p, start, step_rows):
+    def gram_step(p, start, step_rows, keep=False):
         rs = pl.ds(start, step_rows)
         lead, mate = xv[2 * p, rs, :], xv[2 * p + 1, rs, :]
         lh, ll = split(lead)
         mh, ml = split(mate)
+        if keep:
+            for h, hi, lo in ((0, lh, ll), (1, mh, ml)):
+                cols = pl.ds(pl.multiple_of((2 * p + h) * BLK, BLK), BLK)
+                xh_ref[rs, cols] = hi
+                xl_ref[rs, cols] = lo
         gram[p] += mm_t(lh, mh) + (mm_t(lh, ml) + mm_t(ll, mh))
         sq[p, 0] += jnp.sum((lead * lead).reshape(step_rows // 8, 8, BLK), axis=0)
         sq[p, 1] += jnp.sum((mate * mate).reshape(step_rows // 8, 8, BLK), axis=0)
@@ -208,11 +213,6 @@
             qv.at[rnd, p], qv.at[rnd, p], q_s.at[rnd], q_r.at[rnd], device_id=partner, device_id_type=MESH
         )
 
-    def q_out(p):
-        return pltpu.make_async_remote_copy(
-            qv.at[1, p], q_ref.at[p], q_s.at[1], q_r.at[1], device_id=partner, device_id_type=MESH
-        )
-
     def rotate(p, start, step_rows):
         rs = pl.ds(start, step_rows)
         x = jnp.concatenate([xv[2 * p, rs, :], xv[2 * p + 1, rs, :]], axis=1)
@@ -265,12 +265,13 @@
         gram_step(other, start, 2 * unit)
     loads[2].wait()
     loads[3].wait()
-    pl.semaphore_wait(barrier, chips + 2)
-    send_part(0)
     for way, slot in enumerate((up_slot, down_slot)):
         for h in range(2):
             esend[way, h] = xv[(slot // 2) * 2 + h, pl.ds(early, n_early), :]
+    pl.semaphore_wait(barrier, chips + 2)
+    for way in range(2):
         early_copy(way).start()
+    send_part(0)
     for start in range(0, rows, 2 * unit):
         gram_step(core, start, 2 * unit)
     rotation(0, reduce_gram(0))
@@ -300,7 +301,6 @@
 
     gram[...] = jnp.zeros_like(gram)
     sq[...] = jnp.zeros_like(sq)
-    outs = []
 
     def place(start, size, lower, upper):
         rs = pl.ds(start, size)
@@ -308,12 +308,6 @@
             home = origin[j] // 4
             own = nv[jnp.clip(origin[j] - 4 * z, 0, 3), rs, :]
             xv[j, rs, :] = jnp.where(home == z, own, jnp.where(home < z, lower[...], upper[...]))
-            outs.append(
-                pltpu.make_async_copy(
-                    xv.at[j, rs, :], x2_ref.at[rs, j * BLK : (j + 1) * BLK], out_sem.at[len(outs)]
-                )
-            )
-            outs[-1].start()
 
     def arrive(i):
         z_copy(0, i).wait_recv()
@@ -322,8 +316,8 @@
         place(*late[i], zrecv.at[0, rs, :], zrecv.at[1, rs, :])
 
     arrive(0)
-    gram_step(other, *late[0])
-    gram_step(core, *late[0])
+    gram_step(other, *late[0], True)
+    gram_step(core, *late[0], True)
     for k, (t, dev) in enumerate(peers):
         share_gather(k, dev, t).wait_recv()
     share_swap().start()
@@ -337,15 +331,15 @@
         part = qz_other[:, way].reshape(BLK, BLK)
         zearly[way] += mm3(split(erecv[way, other]), split(part))
     place(early, n_early, zearly.at[0], zearly.at[1])
-    gram_step(other, early, n_early)
-    gram_step(core, early, n_early)
+    gram_step(other, early, n_early, True)
+    gram_step(core, early, n_early, True)
     arrive(1)
-    gram_step(other, *late[1])
-    gram_step(core, *late[1])
+    gram_step(other, *late[1], True)
+    gram_step(core, *late[1], True)
     arrive(2)
-    gram_step(other, *late[2])
+    gram_step(other, *late[2], True)
     send_part(1)
-    gram_step(core, *late[2])
+    gram_step(core, *late[2], True)
     for way in range(2):
         for i in range(len(late)):
             z_copy(way, i).wait_send()
@@ -355,27 +349,24 @@
         share_gather(k, dev, chip).wait_send()
     share_swap().wait_send()
     rotation(1, reduce_gram(1))
-    q_out(core).start()
-    final = pltpu.make_async_copy(qv.at[1, core], q_ref.at[core], load_sem.at[0])
-    final.start()
-    for copy in outs:
-        copy.wait()
-    final.wait()
-    q_out(core).wait_send()
-    q_out(other).wait_recv()
+    q_copy(1, core).start()
+    put_rotation([qv[1, core, i] for i in range(3)], qh_ref, ql_ref, core)
+    q_copy(1, core).wait_send()
+    q_copy(1, other).wait_recv()
+    put_rotation([qv[1, other, i] for i in range(3)], qh_ref, ql_ref, other)
 
 
 def two_rounds(plan, x, n_row, n_col):
     rows = x.shape[0]
-    n_early = 3 * rows // 8
+    n_early = rows // 2
     chips = n_row // 2
     crow = BLK // chips
     dma = pltpu.SemaphoreType.DMA
     return pl.pallas_call(
         functools.partial(rounds_kernel, n_row, n_col, rows),
-        out_shape=[jax.ShapeDtypeStruct(x.shape, f32), jax.ShapeDtypeStruct((2, 3, BLK, BLK), f32)],
+        out_shape=[jax.ShapeDtypeStruct(x.shape, bf16)] * 2 + [jax.ShapeDtypeStruct((2, 2 * BLK, 2 * BLK), bf16)] * 2,
         in_specs=[pl.BlockSpec(memory_space=pltpu.SMEM), pl.BlockSpec(memory_space=pl.ANY)],
-        out_specs=[pl.BlockSpec(memory_space=pl.ANY)] * 2,
+        out_specs=[pl.BlockSpec(memory_space=pltpu.VMEM)] * 4,
         scratch_shapes=[
             pltpu.VMEM((4, rows, BLK), f32),
             pltpu.VMEM((4, rows, BLK), f32),
@@ -406,49 +397,40 @@
             dma((2, chips)), dma((2, chips)),
             dma((2,)), dma((2,)),
             dma((2, 3)), dma((2, 3)),
-            dma((16,)),
             dma((2,)), dma((2,)),
             dma((2,)), dma((2,)),
             dma((chips,)), dma((chips,)),
             dma((1,)), dma((1,)),
         ],
-        compiler_params=pltpu.CompilerParams(collective_id=0, has_side_effects=True, vmem_limit_bytes=48 << 20),
+        compiler_params=pltpu.CompilerParams(collective_id=0, has_side_effects=True, vmem_limit_bytes=46 << 20),
     )(plan, x)
 
 
-def rotate_kernel(step_rows, x_ref, q_ref, o_ref, qhi, qlo):
-    @pl.when(pl.program_id(0) == 0)
-    def _():
-        for p in range(2):
-            put_rotation([q_ref[p, i] for i in range(3)], qhi, qlo, p)
-
+def rotate_kernel(step_rows, xh_ref, xl_ref, qh_ref, ql_ref, o_ref):
     rs = pl.ds(pl.multiple_of(pl.program_id(0) * step_rows, step_rows), step_rows)
     for p in range(2):
-        xh, xl = split(x_ref[rs, 2 * p * BLK : (2 * p + 2) * BLK])
+        pair = slice(2 * p * BLK, (2 * p + 2) * BLK)
+        x = xh_ref[rs, pair], xl_ref[rs, pair]
         for h in range(2):
             cols = slice(h * BLK, (h + 1) * BLK)
-            o_ref[:, (2 * p + h) * BLK : (2 * p + h + 1) * BLK] = mm3(
-                (xh, xl), (qhi[p, :, cols], qlo[p, :, cols])
-            )
-
-
-def last_rotation(x, q):
-    rows = x.shape[0]
+            o_ref[:, (2 * p + h) * BLK : (2 * p + h + 1) * BLK] = mm3(x, (qh_ref[p, :, cols], ql_ref[p, :, cols]))
+
+
+def last_rotation(xh, xl, qh, ql):
+    rows = xh.shape[0]
     step_rows = rows // 4
     return pl.pallas_call(
         functools.partial(rotate_kernel, step_rows),
         grid=(rows // step_rows,),
-        out_shape=jax.ShapeDtypeStruct(x.shape, f32),
-        in_specs=[pl.BlockSpec(memory_space=pltpu.VMEM)] * 2,
+        out_shape=jax.ShapeDtypeStruct(xh.shape, f32),
+        in_specs=[pl.BlockSpec(memory_space=pltpu.VMEM)] * 4,
         out_specs=pl.BlockSpec((step_rows, 4 * BLK), lambda i: (i, 0)),
-        scratch_shapes=[pltpu.VMEM((2, 2 * BLK, 2 * BLK), bf16)] * 2,
         compiler_params=pltpu.CompilerParams(vmem_limit_bytes=20 << 20),
-    )(x, q)
+    )(xh, xl, qh, ql)
 
 
 def shards(n_row, n_col, activations, plan):
-    x2, q = two_rounds(plan, activations, n_row, n_col)
-    return last_rotation(x2, q)
+    return last_rotation(*two_rounds(plan, activations, n_row, n_col))
 
 
 def solution(mesh):

time: 80.3 us -> 77.8 us (0.969)
  Pallas kernels: 79.5 us -> 77.1 us
    pallas_call x1, Pallas kernels: 74 us -> 72.1 us  [two_rounds(): pl.pallas_call(functools.partial(rounds_kernel, n_row, n_col, rows), out_...]
where the time goes in v5:
time: 77.8 us
  Pallas kernels  77.1 us (99%)
    pallas_call x1, Pallas kernels, two_rounds(): pl.pallas_call(functools.partial(rounds_kernel, n_row, n_col, rows), out_...  72.1 us
    pallas_call x1, Pallas kernels, last_rotation(): pl.pallas_call(functools.partial(rotate_kernel, step_rows), grid=(rows //...  4.92 us

profile of v5, /device:TPU:1, one launch (start us, length us, event | category | flops | bytes accessed | tf_op | source)
XLA Modules:
  0.0 77.8 jit_solution(16494207012009125346)
XLA Ops:
  0.0 0.0 copy-start
  0.0 0.7 copy-done
  0.7 72.1 %shard_map.28 = (bf16[1024,1024]{1,0:T(8,128)(2,1)S(1)}, bf16[1024,1024]{1,0:T(8,128)(2,1)S(1)}, bf16[2,512,512]{2,1,0:T(8,128)(2,1)S(1)}, bf16[2,512,512]{2,1,0:T(8,128)(2,1)S(1)}) custom-call(s32[2,32]{1,0:T(2,128)S(1)} %copy-done, f32[1024,1024]{1,0:T(8,128)} %x_ref.1), custom_call_target="tpu_custom_call" | custom-call | tf_op jit(solution)/shard_map/pallas_call | solution.py:365
  72.8 4.9 %shard_map.29 = f32[1024,1024]{1,0:T(8,128)} custom-call(bf16[1024,1024]{1,0:T(8,128)(2,1)S(1)} %get-tuple-element.9.xh_ref, bf16[1024,1024]{1,0:T(8,128)(2,1)S(1)} %get-tuple-element.10.xl_ref, bf16[2,512,512]{2,1,0:T(8,128)(2,1)S(1)} %get-tuple-element.11.qh_ref, bf16[2,512,512]{2,1,0:T(8,128)(2,1)S(1)} %get-tuple-element.12.ql_ref), custom_call_target="tpu_custom_call" | custom-call | tf_op jit(solution)/shard_map/pallas_call | solution.py:422
Async XLA Ops:
  0.0 0.7 copy-start

commit v6 on v5

--- a/solution.py
+++ b/solution.py
@@ -45,14 +45,14 @@
     return jnp.where(rows == cols, 1.0, 0.0).astype(f32)
 
 
-def put_rotation(q, hi_ref, lo_ref, pair, whole_ref=None):
-    q11, w, q22 = q
-    for value, r, c in ((q11, 0, 0), (w, 0, 1), (-w.T, 1, 0), (q22, 1, 1)):
-        hi, lo = split(value)
+def put_block(i, value, hi_ref, lo_ref, pair, whole_ref=None):
+    cells = (((value, 0, 0),), ((value, 0, 1), (-value.T, 1, 0)), ((value, 1, 1),))[i]
+    for cell, r, c in cells:
+        hi, lo = split(cell)
         hi_ref[pair, r * BLK : (r + 1) * BLK, c * BLK : (c + 1) * BLK] = hi
         lo_ref[pair, r * BLK : (r + 1) * BLK, c * BLK : (c + 1) * BLK] = lo
         if whole_ref is not None:
-            whole_ref[2 * pair + c, r] = value
+            whole_ref[2 * pair + c, r] = cell
 
 
 def rounds_kernel(
@@ -128,11 +128,10 @@
             part_send.at[rnd], part_recv.at[rnd], part_s.at[rnd], part_r.at[rnd], device_id=partner, device_id_type=MESH
         )
 
-    def send_part(rnd):
+    def fill_part(rnd):
         part_send[rnd, 0:BLK, :] = gram[other, :, 0:HALF]
         part_send[rnd, BLK : 2 * BLK, :] = gram[other, :, HALF:BLK]
         part_send[rnd, 2 * BLK : 2 * BLK + 8, :] = squares(other)
-        part_copy(rnd).start()
 
     def reduce_gram(rnd):
         own_sq = squares(core)
@@ -175,7 +174,7 @@
             ag_copy(k, dev, chip).wait_send()
         return total[2 * crow : 2 * crow + 8]
 
-    def rotation(rnd, sums):
+    def rotation(rnd, sums, *refs):
         lead_sq = jnp.concatenate([sums[0:1], sums[1:2]], axis=1)
         mate_sq = jnp.concatenate([sums[2:3], sums[3:4]], axis=1)
         lead_col = jnp.broadcast_to(lead_sq, (8, BLK)).T[:, 0:1]
@@ -202,15 +201,29 @@
                 res = split(s * square + (1.0 - s) * ident)
         inv_parts = split(inv)
         inv = inv + mm3(inv_parts, split(ident - mm3(split(gmat[...]), inv_parts)))
-        inv = inv + mm3(split(inv), split(ident - full(gmat[...], inv, ((1,), (0,)))))
         w = full(inv, cmat[...], ((1,), (0,)))
-        qv[rnd, core, 0] = 2.0 * inv - ident
-        qv[rnd, core, 1] = w
-        qv[rnd, core, 2] = ident - 0.5 * full(cmat[...], w, ((0,), (0,)))
-
-    def q_copy(rnd, p):
-        return pltpu.make_async_remote_copy(
-            qv.at[rnd, p], qv.at[rnd, p], q_s.at[rnd], q_r.at[rnd], device_id=partner, device_id_type=MESH
+        err = split(ident - full(inv, gmat[...], ((1,), (0,))))
+        inv = inv + mm3(err, split(inv))
+        send_block(rnd, 0, 2.0 * inv - ident, refs)
+        w = w + mm3(err, split(w))
+        send_block(rnd, 1, w, refs)
+        send_block(rnd, 2, ident - 0.5 * full(cmat[...], w, ((0,), (0,))), refs)
+
+    def send_block(rnd, i, value, refs):
+        qv[rnd, core, i] = value
+        q_copy(rnd, core, i).start()
+        put_block(i, value, refs[0], refs[1], core, *refs[2:])
+
+    def receive_blocks(rnd, *refs):
+        for i in range(3):
+            q_copy(rnd, other, i).wait_recv()
+            put_block(i, qv[rnd, other, i], refs[0], refs[1], other, *refs[2:])
+        for i in range(3):
+            q_copy(rnd, core, i).wait_send()
+
+    def q_copy(rnd, p, i):
+        return pltpu.make_async_remote_copy(
+            qv.at[rnd, p, i], qv.at[rnd, p, i], q_s.at[rnd, i], q_r.at[rnd, i], device_id=partner, device_id_type=MESH
         )
 
     def rotate(p, start, step_rows):
@@ -268,20 +281,17 @@
     for way, slot in enumerate((up_slot, down_slot)):
         for h in range(2):
             esend[way, h] = xv[(slot // 2) * 2 + h, pl.ds(early, n_early), :]
-    pl.semaphore_wait(barrier, chips + 2)
-    for way in range(2):
-        early_copy(way).start()
-    send_part(0)
+    fill_part(0)
     for start in range(0, rows, 2 * unit):
         gram_step(core, start, 2 * unit)
-    rotation(0, reduce_gram(0))
-    q_copy(0, core).start()
-    put_rotation([qv[0, core, i] for i in range(3)], qhi, qlo, core, qf)
+    pl.semaphore_wait(barrier, chips + 2)
+    part_copy(0).start()
+    for way in range(2):
+        early_copy(way).start()
+    rotation(0, reduce_gram(0), qhi, qlo, qf)
     for start, size in late:
         rotate(core, start, size)
-    q_copy(0, core).wait_send()
-    q_copy(0, other).wait_recv()
-    put_rotation([qv[0, other, i] for i in range(3)], qhi, qlo, other, qf)
+    receive_blocks(0, qhi, qlo, qf)
     for way, slot in enumerate((up_slot, down_slot)):
         qz[way] = qf[slot, core, pl.ds(pl.multiple_of(chip * crow, crow), crow), :]
         share_copy(way).start()
@@ -326,6 +336,9 @@
     for way in range(2):
         part = qz_all[:, way].reshape(BLK, BLK)
         zearly[way] = mm3(split(erecv[way, core]), split(part))
+    arrive(1)
+    gram_step(other, *late[1], True)
+    gram_step(core, *late[1], True)
     share_swap().wait_recv()
     for way in range(2):
         part = qz_other[:, way].reshape(BLK, BLK)
@@ -333,12 +346,10 @@
     place(early, n_early, zearly.at[0], zearly.at[1])
     gram_step(other, early, n_early, True)
     gram_step(core, early, n_early, True)
-    arrive(1)
-    gram_step(other, *late[1], True)
-    gram_step(core, *late[1], True)
     arrive(2)
     gram_step(other, *late[2], True)
-    send_part(1)
+    fill_part(1)
+    part_copy(1).start()
     gram_step(core, *late[2], True)
     for way in range(2):
         for i in range(len(late)):
@@ -348,12 +359,8 @@
     for k, (_, dev) in enumerate(peers):
         share_gather(k, dev, chip).wait_send()
     share_swap().wait_send()
-    rotation(1, reduce_gram(1))
-    q_copy(1, core).start()
-    put_rotation([qv[1, core, i] for i in range(3)], qh_ref, ql_ref, core)
-    q_copy(1, core).wait_send()
-    q_copy(1, other).wait_recv()
-    put_rotation([qv[1, other, i] for i in range(3)], qh_ref, ql_ref, other)
+    rotation(1, reduce_gram(1), qh_ref, ql_ref)
+    receive_blocks(1, qh_ref, ql_ref)
 
 
 def two_rounds(plan, x, n_row, n_col):
@@ -395,7 +402,7 @@
             dma((2,)), dma((2,)),
             dma((2, chips)), dma((2, chips)),
             dma((2, chips)), dma((2, chips)),
-            dma((2,)), dma((2,)),
+            dma((2, 3)), dma((2, 3)),
             dma((2, 3)), dma((2, 3)),
             dma((2,)), dma((2,)),
             dma((2,)), dma((2,)),

time: 77.8 us -> 76.8 us (0.987)
  Pallas kernels: 77.1 us -> 76 us
    pallas_call x1, Pallas kernels: 72.1 us -> 71.1 us  [two_rounds(): pl.pallas_call(functools.partial(rounds_kernel, n_row, n_col, rows), out_...]
where the time goes in v6:
time: 76.8 us; the launch traced here: 76.7 us
  Pallas kernels  76 us (99%)
    pallas_call x1, Pallas kernels, two_rounds(): pl.pallas_call(functools.partial(rounds_kernel, n_row, n_col, rows), out_...  71.1 us
    pallas_call x1, Pallas kernels, last_rotation(): pl.pallas_call(functools.partial(rotate_kernel, step_rows), grid=(rows //...  4.92 us

profile of v6, /device:TPU:1, one launch (start us, length us, event | category | flops | bytes accessed | tf_op | source)
XLA Modules:
  0.0 76.7 jit_solution(2825577601320703996)
XLA Ops:
  0.0 0.0 copy-start
  0.0 0.7 copy-done
  0.7 71.1 %shard_map.28 = (bf16[1024,1024]{1,0:T(8,128)(2,1)S(1)}, bf16[1024,1024]{1,0:T(8,128)(2,1)S(1)}, bf16[2,512,512]{2,1,0:T(8,128)(2,1)S(1)}, bf16[2,512,512]{2,1,0:T(8,128)(2,1)S(1)}) custom-call(s32[2,32]{1,0:T(2,128)S(1)} %copy-done, f32[1024,1024]{1,0:T(8,128)} %x_ref.1), custom_call_target="tpu_custom_call" | custom-call | tf_op jit(solution)/shard_map/pallas_call | solution.py:372
  71.8 4.9 %shard_map.29 = f32[1024,1024]{1,0:T(8,128)} custom-call(bf16[1024,1024]{1,0:T(8,128)(2,1)S(1)} %get-tuple-element.9.xh_ref, bf16[1024,1024]{1,0:T(8,128)(2,1)S(1)} %get-tuple-element.10.xl_ref, bf16[2,512,512]{2,1,0:T(8,128)(2,1)S(1)} %get-tuple-element.11.qh_ref, bf16[2,512,512]{2,1,0:T(8,128)(2,1)S(1)} %get-tuple-element.12.ql_ref), custom_call_target="tpu_custom_call" | custom-call | tf_op jit(solution)/shard_map/pallas_call | solution.py:429
Async XLA Ops:
  0.0 0.7 copy-start

commit v7 on v6

--- a/solution.py
+++ b/solution.py
@@ -239,7 +239,6 @@
         above, below = plan_ref[1, z_up * 4 + j], plan_ref[1, z_down * 4 + j]
         up_slot = jnp.where(above // 4 == z, above - 4 * z, up_slot)
         down_slot = jnp.where(below // 4 == z, below - 4 * z, down_slot)
-    origin = [plan_ref[1, z * 4 + j] for j in range(4)]
 
     def z_copy(way, i):
         rs = pl.ds(*late[i])
@@ -276,18 +275,18 @@
     loads[1].wait()
     for start in range(0, rows, 2 * unit):
         gram_step(other, start, 2 * unit)
+    fill_part(0)
     loads[2].wait()
     loads[3].wait()
     for way, slot in enumerate((up_slot, down_slot)):
         for h in range(2):
             esend[way, h] = xv[(slot // 2) * 2 + h, pl.ds(early, n_early), :]
-    fill_part(0)
+    pl.semaphore_wait(barrier, chips + 2)
+    for way in range(2):
+        early_copy(way).start()
+    part_copy(0).start()
     for start in range(0, rows, 2 * unit):
         gram_step(core, start, 2 * unit)
-    pl.semaphore_wait(barrier, chips + 2)
-    part_copy(0).start()
-    for way in range(2):
-        early_copy(way).start()
     rotation(0, reduce_gram(0), qhi, qlo, qf)
     for start, size in late:
         rotate(core, start, size)
@@ -312,22 +311,26 @@
     gram[...] = jnp.zeros_like(gram)
     sq[...] = jnp.zeros_like(sq)
 
-    def place(start, size, lower, upper):
+    def place(p, start, size, lower, upper):
         rs = pl.ds(start, size)
-        for j in range(4):
-            home = origin[j] // 4
-            own = nv[jnp.clip(origin[j] - 4 * z, 0, 3), rs, :]
-            xv[j, rs, :] = jnp.where(home == z, own, jnp.where(home < z, lower[...], upper[...]))
+        for h in range(2):
+            origin = plan_ref[1, z * 4 + 2 * p + h]
+            home = origin // 4
+            own = nv[jnp.clip(origin - 4 * z, 0, 3), rs, :]
+            xv[2 * p + h, rs, :] = jnp.where(home == z, own, jnp.where(home < z, lower[...], upper[...]))
+        gram_step(p, start, size, True)
 
     def arrive(i):
         z_copy(0, i).wait_recv()
         z_copy(1, i).wait_recv()
+
+    def place_late(p, i):
         rs = pl.ds(*late[i])
-        place(*late[i], zrecv.at[0, rs, :], zrecv.at[1, rs, :])
+        place(p, *late[i], zrecv.at[0, rs, :], zrecv.at[1, rs, :])
 
     arrive(0)
-    gram_step(other, *late[0], True)
-    gram_step(core, *late[0], True)
+    place_late(other, 0)
+    place_late(core, 0)
     for k, (t, dev) in enumerate(peers):
         share_gather(k, dev, t).wait_recv()
     share_swap().start()
@@ -337,20 +340,19 @@
         part = qz_all[:, way].reshape(BLK, BLK)
         zearly[way] = mm3(split(erecv[way, core]), split(part))
     arrive(1)
-    gram_step(other, *late[1], True)
-    gram_step(core, *late[1], True)
+    place_late(other, 1)
+    place_late(core, 1)
     share_swap().wait_recv()
     for way in range(2):
         part = qz_other[:, way].reshape(BLK, BLK)
         zearly[way] += mm3(split(erecv[way, other]), split(part))
-    place(early, n_early, zearly.at[0], zearly.at[1])
-    gram_step(other, early, n_early, True)
-    gram_step(core, early, n_early, True)
+    place(other, early, n_early, zearly.at[0], zearly.at[1])
+    place(core, early, n_early, zearly.at[0], zearly.at[1])
     arrive(2)
-    gram_step(other, *late[2], True)
+    place_late(other, 2)
     fill_part(1)
     part_copy(1).start()
-    gram_step(core, *late[2], True)
+    place_late(core, 2)
     for way in range(2):
         for i in range(len(late)):
             z_copy(way, i).wait_send()

time: 76.8 us -> 76.6 us (level)
  no operation moved by 1% of the time
where the time goes in v7:
time: 76.6 us; the launch traced here: 76.5 us
  Pallas kernels  75.8 us (99%)
    pallas_call x1, Pallas kernels, two_rounds(): pl.pallas_call(functools.partial(rounds_kernel, n_row, n_col, rows), out_...  70.9 us
    pallas_call x1, Pallas kernels, last_rotation(): pl.pallas_call(functools.partial(rotate_kernel, step_rows), grid=(rows //...  4.92 us

profile of v7, /device:TPU:1, one launch (start us, length us, event | category | flops | bytes accessed | tf_op | source)
XLA Modules:
  0.0 76.5 jit_solution(5895818650931847969)
XLA Ops:
  0.0 0.0 copy-start
  0.0 0.7 copy-done
  0.7 70.9 %shard_map.28 = (bf16[1024,1024]{1,0:T(8,128)(2,1)S(1)}, bf16[1024,1024]{1,0:T(8,128)(2,1)S(1)}, bf16[2,512,512]{2,1,0:T(8,128)(2,1)S(1)}, bf16[2,512,512]{2,1,0:T(8,128)(2,1)S(1)}) custom-call(s32[2,32]{1,0:T(2,128)S(1)} %copy-done, f32[1024,1024]{1,0:T(8,128)} %x_ref.1), custom_call_target="tpu_custom_call" | custom-call | tf_op jit(solution)/shard_map/pallas_call | solution.py:374
  71.6 4.9 %shard_map.29 = f32[1024,1024]{1,0:T(8,128)} custom-call(bf16[1024,1024]{1,0:T(8,128)(2,1)S(1)} %get-tuple-element.9.xh_ref, bf16[1024,1024]{1,0:T(8,128)(2,1)S(1)} %get-tuple-element.10.xl_ref, bf16[2,512,512]{2,1,0:T(8,128)(2,1)S(1)} %get-tuple-element.11.qh_ref, bf16[2,512,512]{2,1,0:T(8,128)(2,1)S(1)} %get-tuple-element.12.ql_ref), custom_call_target="tpu_custom_call" | custom-call | tf_op jit(solution)/shard_map/pallas_call | solution.py:431
Async XLA Ops:
  0.0 0.7 copy-start

commit v8 on v7

--- a/solution.py
+++ b/solution.py
@@ -71,7 +71,7 @@
     partner = (chip * 2 + other, z)
     z_up, z_down = lax.rem(z + 1, n_col), lax.rem(z + n_col - 1, n_col)
     unit = rows // 8
-    late = [(0, 2 * unit), (2 * unit, unit), (3 * unit, unit)]
+    late = [(0, unit), (unit, 2 * unit), (3 * unit, unit)]
     early, n_early = 4 * unit, 4 * unit
 
     side = math.isqrt(chips)

time: 76.6 us -> 76.7 us (level)
  no operation moved by 1% of the time
where the time goes in v8:
time: 76.7 us; the launch traced here: 76.6 us
  Pallas kernels  75.9 us (99%)
    pallas_call x1, Pallas kernels, two_rounds(): pl.pallas_call(functools.partial(rounds_kernel, n_row, n_col, rows), out_...  71 us
    pallas_call x1, Pallas kernels, last_rotation(): pl.pallas_call(functools.partial(rotate_kernel, step_rows), grid=(rows //...  4.92 us

profile of v8, /device:TPU:1, one launch (start us, length us, event | category | flops | bytes accessed | tf_op | source)
XLA Modules:
  0.0 76.6 jit_solution(6703880813901226724)
XLA Ops:
  0.0 0.0 copy-start
  0.0 0.7 copy-done
  0.7 71.0 %shard_map.28 = (bf16[1024,1024]{1,0:T(8,128)(2,1)S(1)}, bf16[1024,1024]{1,0:T(8,128)(2,1)S(1)}, bf16[2,512,512]{2,1,0:T(8,128)(2,1)S(1)}, bf16[2,512,512]{2,1,0:T(8,128)(2,1)S(1)}) custom-call(s32[2,32]{1,0:T(2,128)S(1)} %copy-done, f32[1024,1024]{1,0:T(8,128)} %x_ref.1), custom_call_target="tpu_custom_call" | custom-call | tf_op jit(solution)/shard_map/pallas_call | solution.py:374
  71.7 4.9 %shard_map.29 = f32[1024,1024]{1,0:T(8,128)} custom-call(bf16[1024,1024]{1,0:T(8,128)(2,1)S(1)} %get-tuple-element.9.xh_ref, bf16[1024,1024]{1,0:T(8,128)(2,1)S(1)} %get-tuple-element.10.xl_ref, bf16[2,512,512]{2,1,0:T(8,128)(2,1)S(1)} %get-tuple-element.11.qh_ref, bf16[2,512,512]{2,1,0:T(8,128)(2,1)S(1)} %get-tuple-element.12.ql_ref), custom_call_target="tpu_custom_call" | custom-call | tf_op jit(solution)/shard_map/pallas_call | solution.py:431
Async XLA Ops:
  0.0 0.7 copy-start

commit v9 on v7

--- a/solution.py
+++ b/solution.py
@@ -353,6 +353,7 @@
     fill_part(1)
     part_copy(1).start()
     place_late(core, 2)
+    rotation(1, reduce_gram(1), qh_ref, ql_ref)
     for way in range(2):
         for i in range(len(late)):
             z_copy(way, i).wait_send()
@@ -361,7 +362,6 @@
     for k, (_, dev) in enumerate(peers):
         share_gather(k, dev, chip).wait_send()
     share_swap().wait_send()
-    rotation(1, reduce_gram(1), qh_ref, ql_ref)
     receive_blocks(1, qh_ref, ql_ref)
 
 

time: 76.6 us -> 76.6 us (level)
  no operation moved by 1% of the time
where the time goes in v9:
time: 76.6 us; the launch traced here: 76.5 us
  Pallas kernels  75.8 us (99%)
    pallas_call x1, Pallas kernels, two_rounds(): pl.pallas_call(functools.partial(rounds_kernel, n_row, n_col, rows), out_...  70.9 us
    pallas_call x1, Pallas kernels, last_rotation(): pl.pallas_call(functools.partial(rotate_kernel, step_rows), grid=(rows //...  4.92 us

profile of v9, /device:TPU:1, one launch (start us, length us, event | category | flops | bytes accessed | tf_op | source)
XLA Modules:
  0.0 76.5 jit_solution(9984378779097791518)
XLA Ops:
  0.0 0.0 copy-start
  0.0 0.7 copy-done
  0.7 70.9 %shard_map.28 = (bf16[1024,1024]{1,0:T(8,128)(2,1)S(1)}, bf16[1024,1024]{1,0:T(8,128)(2,1)S(1)}, bf16[2,512,512]{2,1,0:T(8,128)(2,1)S(1)}, bf16[2,512,512]{2,1,0:T(8,128)(2,1)S(1)}) custom-call(s32[2,32]{1,0:T(2,128)S(1)} %copy-done, f32[1024,1024]{1,0:T(8,128)} %x_ref.1), custom_call_target="tpu_custom_call" | custom-call | tf_op jit(solution)/shard_map/pallas_call | solution.py:374
  71.6 4.9 %shard_map.29 = f32[1024,1024]{1,0:T(8,128)} custom-call(bf16[1024,1024]{1,0:T(8,128)(2,1)S(1)} %get-tuple-element.9.xh_ref, bf16[1024,1024]{1,0:T(8,128)(2,1)S(1)} %get-tuple-element.10.xl_ref, bf16[2,512,512]{2,1,0:T(8,128)(2,1)S(1)} %get-tuple-element.11.qh_ref, bf16[2,512,512]{2,1,0:T(8,128)(2,1)S(1)} %get-tuple-element.12.ql_ref), custom_call_target="tpu_custom_call" | custom-call | tf_op jit(solution)/shard_map/pallas_call | solution.py:431
Async XLA Ops:
  0.0 0.7 copy-start
